TPU v7x, 256 devices: a whole 4x4x8 slice. The times are simulated.
256 devices in a mesh: rep: 4 (over x), table: 64 (over z, y, core).
Axes of the slice: x: 4, y: 4, z: 8, core: 2. Of those that a mesh axis runs over, the one named last changes fastest.
Arguments:
- cold_table: float32 [65536, 400], P('table'), may hold values from -3 to 3
- cold_state: float32 [65536], P('table'), may hold values from 0.05 to 1
- hot_table: float32 [8192, 400], P('table'), may hold values from -3 to 3
- hot_state: float32 [8192], P('table'), may hold values from 0.05 to 1
- relations: float32 [512, 400], replicated, may hold values from -2.5 to 2.5
- head_owner: int32 [131072, 1], P(('rep', 'table')), may hold values from 0 to 63; in each aligned block of 512 rows (0 to 511, 512 to 1023, ...) at most 16 rows name the same one
- head_row: int32 [131072], P(('rep', 'table')), may hold values from 0 to 1023
- edge_rel: int32 [131072], P(('rep', 'table')), may hold values from 0 to 511
- edge_tail: int32 [131072], P(('rep', 'table')), may hold values from 0 to 8191, as said below
- neg_ids: int32 [4, 512], P('rep', 'table'), may hold values from 0 to 1023
Outputs:
- new_cold_table: float32 [65536, 400], P('table')
- new_cold_state: float32 [65536], P('table')
- new_hot_table: float32 [8192, 400], P('table')
- new_hot_state: float32 [8192], P('table')
Inputs may be any that keep to these rules, and one draw needn't show every extreme that they name: `head_owner`: among the edges of one device (aligned blocks of 512), no owner is named more than 16 times. `neg_ids`: column j names a row of the cold rows of table index j // 8. `edge_tail`: among the edges of one device (aligned blocks of 512), the tails that lie in one aligned block of 128 hot rows are at most 32 distinct rows, and in some such block exactly 32.
All inputs are finite; a program needn't handle non-finite values.
Results may differ from a plain program's by a relative error of at most 0.00045.
The roundings to bfloat16 on the way count: a program that leaves them out, or rounds other values in their place, can miss the bound.
Values may be sent and summed in bfloat16 or wider, within the bound.
No kernel may reach another device: no remote copies, remote signals or barrier semaphores. Data moves between devices by JAX's collectives and lax.ppermute only.
A program may use at most 128 MiB of HBM per device.

v0:
```python
import functools
import jax
import jax.numpy as jnp
from jax import lax
from jax.experimental import pallas as pl
from jax.experimental.pallas import tpu as pltpu
from jax.sharding import PartitionSpec as P


learn_rate = 0.5
HEAD_CAP = 16
TAIL_CAP = 32
GROUP = 8
HALF = 256
FULL = 2 * HALF

BF = jnp.bfloat16
I16 = jnp.int16
F32 = jnp.float32
I32 = jnp.int32


def dot(a, b, dims):
    return lax.dot_general(a, b, (dims, ((), ())), preferred_element_type=F32)


MM = ((1,), (0,))
NT = ((1,), (1,))
TN = ((0,), (0,))


def one_hot(ids, count):
    return (ids[:, None] == lax.broadcasted_iota(I32, (1, count), 1)).astype(BF)


def widen(rows):
    half = rows.shape[-1] // 2
    pad = [(0, 0)] * (rows.ndim - 1) + [(0, HALF - half)]
    return jnp.concatenate([jnp.pad(rows[..., :half], pad), jnp.pad(rows[..., half:], pad)], -1)


def narrow(rows, width):
    half = width // 2
    return jnp.concatenate([rows[..., :half], rows[..., HALF : HALF + half]], -1)


def mask_of(shape, ids_row, base=0):
    return (lax.broadcasted_iota(I32, shape, 0) + base == ids_row).astype(BF)


def two_part_dot(mask, x, dims=MM):
    hi = x.astype(BF)
    lo = (x - hi.astype(F32)).astype(BF)
    return dot(mask, hi, dims) + dot(mask, lo, dims)


def packed(x):
    peak = jnp.max(jnp.abs(x), axis=-1, keepdims=True)
    power = jnp.floor(jnp.log(jnp.maximum(peak, 1e-30)) * 1.4426950408889634)
    code = jnp.round(x * jnp.exp2(14.0 - power))
    lane = lax.broadcasted_iota(I32, x.shape, x.ndim - 1)
    code = jnp.where(lane >= FULL - 8, power, jnp.clip(code, -32767.0, 32767.0))
    return code.astype(I32).astype(I16)


def unpacked(code):
    x = code.astype(F32)
    lane = lax.broadcasted_iota(I32, x.shape, x.ndim - 1)
    scale = jnp.exp2(x[..., FULL - 1 :] - 14.0)
    return jnp.where(lane >= FULL - 8, 0.0, x * scale)


def with_rel(rel, v):
    v_re, v_im, r_re, r_im = v[:, :HALF], v[:, HALF:], rel[:, :HALF], rel[:, HALF:]
    return jnp.concatenate([v_re * r_re - v_im * r_im, v_re * r_im + v_im * r_re], axis=1)


def against_rel(rel, v):
    v_re, v_im, r_re, r_im = v[:, :HALF], v[:, HALF:], rel[:, :HALF], rel[:, HALF:]
    return jnp.concatenate([r_re * v_re + r_im * v_im, r_re * v_im - r_im * v_re], axis=1)


def put(ref, value):
    ref[...] = value


def edge_kernel(slot_col, slot_row, tail_col, tail_row, rel_ref, rows_ref, *refs):
    pieces, (same_msg, other_msg, back_msg) = refs[:5], refs[5:8]
    found, negs, hi_buf, lo_buf, head_buf, neg_buf = refs[8:]
    edges = slot_col.shape[0]
    slots = rows_ref.shape[0]
    part = found.shape[0] // GROUP
    per = slots // (GROUP * GROUP)
    n_neg = negs.shape[0]
    found[:part, :] = pieces[0][:part, :]
    found[part : 2 * part, :] = pieces[1][:part, :]
    for y in range(1, GROUP // 2):
        found[2 * y * part : 2 * (y + 1) * part, :] = pieces[y + 1][...]
    halves = 2
    e_half, s_half, n_half = edges // halves, slots // halves, n_neg // halves
    j = lax.broadcasted_iota(I32, (n_half, 1), 0)
    neg_col = (j >> 3) * per + HEAD_CAP + (j & 7)
    j = lax.broadcasted_iota(I32, (1, n_half), 1)
    neg_row = (j >> 3) * per + HEAD_CAP + (j & 7)

    @pl.loop(0, halves)
    def _(c):
        at = pl.ds(pl.multiple_of(c * s_half, s_half), s_half)
        pick = (neg_col == lax.broadcasted_iota(I32, (n_half, s_half), 1)).astype(BF)
        to = pl.ds(pl.multiple_of(c * n_half, n_half), n_half)
        negs[to, :] = dot(pick, rows_ref[at, :], MM).astype(BF)

    neg_buf[...] = jnp.zeros_like(neg_buf)

    @pl.loop(0, halves)
    def _(h):
        at = pl.ds(pl.multiple_of(h * e_half, e_half), e_half)
        rel = rel_ref[at, :]
        pick = tail_col[at, :] == lax.broadcasted_iota(I32, (e_half, GROUP * part), 1)
        tail_f = dot(pick.astype(BF), found[...], MM)
        pick = slot_col[at, :] == lax.broadcasted_iota(I32, (e_half, slots), 1)
        head_f = dot(pick.astype(BF), rows_ref[...], MM)
        negatives = negs[...]
        queries = with_rel(rel, head_f)
        probes = against_rel(rel, tail_f)
        positive = jnp.sum(queries * tail_f, axis=1, keepdims=True)
        query_b = queries.astype(BF)
        probe_b = probes.astype(BF)
        pos_weight = -jax.nn.sigmoid(-positive)
        tail_weight = jax.nn.sigmoid(dot(query_b, negatives, NT)).astype(BF)
        head_weight = jax.nn.sigmoid(dot(probe_b, negatives, NT)).astype(BF)
        tail_mix = dot(tail_weight, negatives, MM)
        head_mix = dot(head_weight, negatives, MM)
        head_buf[at, :] = against_rel(rel, pos_weight * tail_f + tail_mix).astype(BF)
        tail_grad = with_rel(rel, pos_weight * head_f + head_mix)
        grad_hi = tail_grad.astype(BF)
        hi_buf[at, :] = grad_hi
        lo_buf[at, :] = (tail_grad - grad_hi.astype(F32)).astype(BF)
        neg_buf[...] += dot(tail_weight, query_b, TN) + dot(head_weight, probe_b, TN)

    @pl.loop(0, GROUP)
    def _(k):
        mask = mask_of((part, edges), tail_row[...], k * part)
        code = packed(dot(mask, hi_buf[...], MM) + dot(mask, lo_buf[...], MM))
        at = pl.ds(pl.multiple_of((k >> 1) * part, part), part)
        pl.when((k & 1) == 0)(functools.partial(put, same_msg.at[at], code))
        pl.when((k & 1) == 1)(functools.partial(put, other_msg.at[at], code))

    @pl.loop(0, halves)
    def _(c):
        to = pl.ds(pl.multiple_of(c * s_half, s_half), s_half)
        back = dot(mask_of((s_half, edges), slot_row[...], c * s_half), head_buf[...], MM)
        grads = neg_buf[pl.ds(pl.multiple_of(c * n_half, n_half), n_half), :]
        back = back + two_part_dot(mask_of((s_half, n_half), neg_row), grads)
        back_msg[to, :] = packed(back)


def edge_call(head_slot, tail_slot, rel, rows, pieces):
    edges = head_slot.shape[0]
    slots = rows.shape[0]
    part = pieces[1].shape[0] * 2 // GROUP
    n_neg = slots - GROUP * GROUP * HEAD_CAP
    outs = pl.pallas_call(
        edge_kernel,
        in_specs=[vmem()] * (6 + len(pieces)),
        out_specs=[vmem()] * 3,
        out_shape=[jax.ShapeDtypeStruct((GROUP // 2 * part, FULL), I16)] * 2
        + [jax.ShapeDtypeStruct((slots, FULL), I16)],
        scratch_shapes=[
            pltpu.VMEM((GROUP * part, FULL), BF),
            pltpu.VMEM((n_neg, FULL), BF),
            pltpu.VMEM((edges, FULL), BF),
            pltpu.VMEM((edges, FULL), BF),
            pltpu.VMEM((edges, FULL), BF),
            pltpu.VMEM((n_neg, FULL), F32),
        ],
        cost_estimate=pl.CostEstimate(flops=9 << 30, bytes_accessed=16 << 20, transcendentals=1 << 20),
        name="edge",
    )(
        head_slot[:, None],
        head_slot[None, :],
        tail_slot[:, None],
        tail_slot[None, :],
        rel,
        rows,
        *pieces,
    )
    return outs


def answer_kernel(me_ref, ids_ref, here, behind, ahead, same_out, other_out):
    n_ring = ids_ref.shape[0]
    rows = here.shape[0] // 3
    places = ((here, 1), (here, 0), (behind, 2), (behind, 1), (behind, 0), (ahead, 1), (ahead, 0), (here, 2))
    for k, (ref, i) in enumerate(places):
        z = lax.rem(me_ref[0] - k + n_ring, n_ring)
        mask = mask_of((rows, GROUP * TAIL_CAP), ids_ref[pl.ds(z, 1), :])
        found = dot(mask, ref[i * rows : (i + 1) * rows, :], TN).astype(BF)
        for g in range(GROUP):
            start = pl.multiple_of((g // 2) * n_ring * TAIL_CAP + z * TAIL_CAP, TAIL_CAP)
            out = other_out if g % 2 else same_out
            out[pl.ds(start, TAIL_CAP), :] = found[g * TAIL_CAP : (g + 1) * TAIL_CAP, :]


def answer_call(ring_me, ids, blocks):
    n_ring = ids.shape[0]
    out = jax.ShapeDtypeStruct((GROUP // 2 * n_ring * TAIL_CAP, FULL), BF)
    return pl.pallas_call(
        answer_kernel,
        in_specs=[smem()] + [vmem()] * (1 + len(blocks)),
        out_specs=[vmem()] * 2,
        out_shape=[out] * 2,
        cost_estimate=pl.CostEstimate(flops=1 << 30, bytes_accessed=4 << 20, transcendentals=0),
        name="answer",
    )(ring_me, ids, *blocks)


def coded_parts(src, own_ref, msgs, me, n_rep):
    @pl.loop(0, n_rep)
    def _(k):
        part = src(lax.rem(me + k, n_rep))
        pl.when(k == 0)(functools.partial(put, own_ref, part))
        code = packed(part)
        for step in range(1, n_rep):
            pl.when(k == step)(functools.partial(put, msgs[step - 1], code))


def dense_kernel(me_ref, ids_ref, *refs, n_rep):
    got, own_ref, msgs, dense = refs[:5], refs[5], refs[6:-1], refs[-1]
    n_ring, rows, _ = dense.shape

    @pl.loop(0, n_ring)
    def _(z):
        at = pl.ds(pl.multiple_of(z * TAIL_CAP, TAIL_CAP), TAIL_CAP)
        then = pl.ds(pl.multiple_of((n_ring + z) * TAIL_CAP, TAIL_CAP), TAIL_CAP)
        part = [got[0][at, :], got[1][at, :]]
        for pair in got[2:]:
            part += [pair[at, :], pair[then, :]]
        part = [unpacked(code) for code in part]
        mask = mask_of((rows, GROUP * TAIL_CAP), ids_ref[pl.ds(z, 1), :])
        dense[z] = two_part_dot(mask, jnp.concatenate(part, axis=0))

    quarter = rows // n_rep

    def src(q):
        start = pl.multiple_of(q * quarter, quarter)
        return dense[:, pl.ds(start, quarter), :].reshape(n_ring * quarter, FULL)

    coded_parts(src, own_ref, msgs, me_ref[0], n_rep)


def cold_kernel(me_ref, ids_ref, neg_ref, back_ref, own_ref, *refs, n_rep):
    n_src, per, _ = back_ref.shape
    msgs, flat = refs[:-1], refs[-1]
    quarter = own_ref.shape[0]
    back = unpacked(back_ref[...])
    negs = per - HEAD_CAP
    neg_sum = jnp.sum(back[:, HEAD_CAP:, :], axis=0)
    flat[...] = back.reshape(n_src * per, FULL).astype(BF)
    hi = neg_sum.astype(BF)
    rest = neg_sum - hi.astype(F32)

    def src(q):
        mask = mask_of((quarter, n_src * per), ids_ref[...], q * quarter)
        neg_mask = mask_of((quarter, negs), neg_ref[...], q * quarter)
        return dot(mask, flat[...], MM) + dot(neg_mask, hi, MM) + two_part_dot(neg_mask, rest)

    coded_parts(src, own_ref, msgs, me_ref[0], n_rep)


def smem():
    return pl.BlockSpec(memory_space=pltpu.SMEM)


def vmem():
    return pl.BlockSpec(memory_space=pltpu.VMEM)


def parts_call(kernel, me, operands, rows, scratch, n_rep):
    return pl.pallas_call(
        functools.partial(kernel, n_rep=n_rep),
        in_specs=[smem()] + [vmem()] * len(operands),
        out_specs=[vmem()] * n_rep,
        out_shape=[jax.ShapeDtypeStruct((rows, FULL), F32)]
        + [jax.ShapeDtypeStruct((rows, FULL), I16)] * (n_rep - 1),
        scratch_shapes=[scratch],
        cost_estimate=pl.CostEstimate(flops=4 << 30, bytes_accessed=8 << 20, transcendentals=0),
    )(me, *operands)


def shift(x, step, n_rep):
    return lax.ppermute(x, "rep", [(i, (i + step) % n_rep) for i in range(n_rep)])


def ring_shift(x, step, n_table):
    return lax.ppermute(x, "table", [(i, (i + step * GROUP) % n_table) for i in range(n_table)])


def near_swap(x, other, n_table):
    return lax.ppermute(x, "table", [(i, i ^ other) for i in range(n_table)])


def near_exchange(same, other, n_table):
    swapped = near_swap(other, 1, n_table)
    got = [same, swapped]
    size = same.shape[0] // (GROUP // 2)
    for y in range(1, GROUP // 2):
        at = slice(y * size, (y + 1) * size)
        got.append(near_swap(jnp.concatenate([same[at], swapped[at]]), 2 * y, n_table))
    return got


def sum_kernel(own_ref, *refs):
    got, out_ref = refs[:-1], refs[-1]
    total = own_ref[...]
    for part in got:
        total = total + unpacked(part[...])
    out_ref[...] = packed(total) if out_ref.dtype == I16 else total


def sum_call(own, got, dtype):
    return pl.pallas_call(
        sum_kernel,
        in_specs=[vmem()] * (1 + len(got)),
        out_specs=vmem(),
        out_shape=jax.ShapeDtypeStruct(own.shape, dtype),
    )(own, *got)


def update_kernel(me_ref, table_ref, state_ref, *refs):
    parts, table_out, state_out = refs[:-2], refs[-2], refs[-1]
    n_rep = len(parts)
    half = table_ref.shape[0] // 2
    for k in range(n_rep):
        quarter = parts[k].shape[0]
        q = lax.rem(me_ref[0] - k + n_rep, n_rep)
        at = pl.ds(pl.multiple_of(q * quarter, quarter), quarter)
        grad = unpacked(parts[k][...]).T
        grad = jnp.concatenate([grad[:half], grad[HALF : HALF + half]], axis=0)
        state = state_ref[:, at] + jnp.sum(grad * grad, axis=0, keepdims=True) / (2 * half)
        state_out[:, at] = state
        table_out[:, at] = table_ref[:, at] - learn_rate * grad / jnp.sqrt(state)


def cold_update(me, table, state, parts):
    rows, width = table.shape
    new_table, new_state = pl.pallas_call(
        update_kernel,
        in_specs=[smem()] + [vmem()] * (2 + len(parts)),
        out_specs=[vmem()] * 2,
        out_shape=[
            jax.ShapeDtypeStruct((width, rows), F32),
            jax.ShapeDtypeStruct((1, rows), F32),
        ],
        name="update",
    )(me, table.T, state[None, :], *parts)
    return new_table.T, new_state[0]


def pick_kernel(ids_ref, table_ref, out_ref):
    rows = table_ref.shape[0]
    slots = out_ref.shape[0]
    step = 512

    @pl.loop(0, slots // step)
    def _(c):
        at = pl.ds(pl.multiple_of(c * step, step), step)
        out_ref[at, :] = dot(mask_of((rows, step), ids_ref[:, at]), table_ref[...], TN).astype(BF)


def pick_call(ids, table):
    slots = ids.shape[1]
    return pl.pallas_call(
        pick_kernel,
        in_specs=[vmem()] * 2,
        out_specs=vmem(),
        out_shape=jax.ShapeDtypeStruct((slots, FULL), BF),
        cost_estimate=pl.CostEstimate(flops=2 << 30, bytes_accessed=3 << 20, transcendentals=0),
        name="pick",
    )(ids, table)


def adagrad(weights, state, grad):
    new_state = state + jnp.mean(grad * grad, axis=1)
    return (weights - learn_rate * grad / jnp.sqrt(new_state)[:, None], new_state)


def per_device(
    cold_table,
    cold_state,
    hot_table,
    hot_state,
    relations,
    head_owner,
    head_row,
    edge_rel,
    edge_tail,
    neg_ids,
):
    n_table = lax.axis_size("table")
    n_rep = lax.axis_size("rep")
    n_ring = n_table // GROUP
    edges = head_row.shape[0]
    width = cold_table.shape[1]
    cold_rows = cold_table.shape[0]
    hot_rows = hot_table.shape[0]
    negs = neg_ids.shape[1]
    near = [[z * GROUP + g for g in range(GROUP)] for z in range(n_ring)]
    far = [[z * GROUP + g for z in range(n_ring)] for g in range(GROUP)]

    per = HEAD_CAP + negs
    me = lax.axis_index("rep").astype(I32).reshape(1)

    place = lax.axis_index("table").astype(I32)
    ring_me, near_me = (place // GROUP).reshape(1), place % GROUP

    hot_bf = widen(hot_table.astype(BF))
    before_us = ring_shift(hot_bf, 1, n_table)
    after_us = ring_shift(hot_bf, n_ring - 1, n_table)
    here = jnp.concatenate([before_us, hot_bf, after_us])
    behind = ring_shift(here, 3, n_table)
    ahead = ring_shift(here, n_ring - 3, n_table)
    cold_bf = widen(cold_table.astype(BF))

    owner_hot = one_hot(head_owner[:, 0], n_table)
    row = lax.broadcasted_iota(jnp.int32, (edges, edges), 0)
    col = lax.broadcasted_iota(jnp.int32, (edges, edges), 1)
    before = dot((col < row).astype(BF), owner_hot, ((1,), (0,)))
    rank = jnp.sum(before * owner_hot.astype(F32), axis=1).astype(jnp.int32)
    head_slot = head_owner[:, 0] * per + rank

    block = edge_tail // hot_rows
    within = edge_tail % hot_rows
    block_hot = one_hot(block, n_table)
    within_hot = one_hot(within, hot_rows)
    present = (dot(block_hot, within_hot, ((0,), (0,))) > 0.5).astype(BF)
    prow = lax.broadcasted_iota(jnp.int32, (hot_rows, hot_rows), 0)
    pcol = lax.broadcasted_iota(jnp.int32, (hot_rows, hot_rows), 1)
    ranks = dot(present, (prow < pcol).astype(BF), ((1,), (0,)))
    rank_of = dot(block_hot, ranks.astype(BF), ((1,), (0,)))
    tail_rank = jnp.sum(rank_of * within_hot.astype(F32), axis=1).astype(jnp.int32)
    z_of, g_of = block // GROUP, block % GROUP
    tail_slot = ((g_of ^ near_me) * n_ring + z_of) * TAIL_CAP + tail_rank
    slot_iota = lax.broadcasted_iota(jnp.int32, (n_table, hot_rows, TAIL_CAP), 2)
    match = (ranks.astype(jnp.int32)[:, :, None] == slot_iota) & (present > 0.5)[:, :, None]
    row_iota = lax.broadcasted_iota(jnp.int32, (n_table, hot_rows, TAIL_CAP), 1) + 1
    slot_rows = jnp.sum(jnp.where(match, row_iota, 0), axis=1) - 1
    slot_rows = slot_rows.reshape(n_ring, GROUP, TAIL_CAP).transpose(1, 0, 2)

    wanted = jnp.zeros((n_table * per,), I32).at[head_slot].set(head_row).reshape(n_table, per)
    wanted = lax.all_to_all(wanted[:, :HEAD_CAP], "table", 0, 0)
    dense_rows = lax.all_to_all(
        slot_rows.reshape(GROUP, n_ring * TAIL_CAP), "table", 0, 0, axis_index_groups=near
    )
    dense_ids = dense_rows.reshape(GROUP, n_ring, TAIL_CAP)[jnp.arange(GROUP) ^ near_me]
    dense_ids = dense_ids.transpose(1, 0, 2).reshape(n_ring, GROUP * TAIL_CAP)
    own_negs = jnp.broadcast_to(neg_ids[0][None, :], (n_table, negs))
    asked = jnp.concatenate([wanted, own_negs], axis=1)
    head_ids = jnp.concatenate([wanted, jnp.full((n_table, negs), -1, I32)], axis=1)
    picked = pick_call(asked.reshape(1, n_table * per), cold_bf)
    rows = lax.all_to_all(picked.reshape(n_table, per, FULL), "table", 0, 0)
    relation = widen(relations[edge_rel])
    found = answer_call(ring_me, dense_ids, (here, behind, ahead))
    pieces = near_exchange(*found, n_table)
    same_msg, other_msg, back_msg = edge_call(
        head_slot, tail_slot, relation, rows.reshape(n_table * per, FULL), pieces
    )

    back = lax.all_to_all(back_msg.reshape(n_table, per, FULL), "table", 0, 0)
    tail_got = near_exchange(same_msg, other_msg, n_table)

    quarter = hot_rows // n_rep
    hot_own, *hot_msg = parts_call(
        dense_kernel,
        me,
        (dense_ids, *tail_got),
        n_ring * quarter,
        pltpu.VMEM((n_ring, hot_rows, FULL), F32),
        n_rep,
    )
    hot_got = [shift(hot_msg[k - 1], k, n_rep) for k in range(1, n_rep)]
    cold_own, *cold_msg = parts_call(
        cold_kernel,
        me,
        (head_ids.reshape(1, n_table * per), neg_ids, back),
        cold_rows // n_rep,
        pltpu.VMEM((n_table * per, FULL), BF),
        n_rep,
    )
    cold_got = []
    for k in range(1, n_rep):
        cold_got.append(shift(cold_msg[k - 1], k, n_rep))
    hot_own, _ = lax.optimization_barrier((hot_own, cold_own))
    hot_part = sum_call(hot_own, hot_got, F32)
    hot_rows_got = lax.all_to_all(
        hot_part.reshape(n_ring, quarter, FULL), "table", 0, 0, axis_index_groups=far
    )
    cold_part = sum_call(cold_own, cold_got, I16)
    cold_parts = [cold_part] + [shift(cold_part, k, n_rep) for k in range(1, n_rep)]
    hot_sum = jnp.sum(hot_rows_got, axis=0)
    new_cold_table, new_cold_state = cold_update(me, cold_table, cold_state, cold_parts)

    hot_parts = [hot_sum]
    for k in range(1, n_rep):
        hot_parts.append(shift(hot_sum, k, n_rep))
    hot_total = jnp.zeros((n_rep, quarter, FULL), F32)
    for k, part in enumerate(hot_parts):
        hot_total = lax.dynamic_update_index_in_dim(
            hot_total, part, lax.rem(me[0] - k + n_rep, n_rep), 0
        )
    hot_total = narrow(hot_total.reshape(hot_rows, FULL), width)
    new_hot_table, new_hot_state = adagrad(hot_table, hot_state, hot_total)
    return (new_cold_table, new_cold_state, new_hot_table, new_hot_state)


def solution(mesh):
    in_specs = (
        P("table", None),
        P("table"),
        P("table", None),
        P("table"),
        P(),
        P(("rep", "table"), None),
        P(("rep", "table")),
        P(("rep", "table")),
        P(("rep", "table")),
        P("rep", "table"),
    )
    out_specs = (P("table", None), P("table"), P("table", None), P("table"))

    return jax.shard_map(
        per_device, mesh=mesh, in_specs=in_specs, out_specs=out_specs, check_vma=False
    )
```

profile of v0, /device:TPU:1, one launch (start us, length us, event | category | flops | bytes accessed | tf_op | source)
XLA Modules:
  0.0 299.2 jit_solution(4374944418038944149)
XLA Ops:
  2.7 6.5 %collective-permute-start.1 = (bf16[128,512]{1,0:T(8,128)(2,1)S(1)}, bf16[128,512]{1,0:T(8,128)(2,1)S(1)}, u32[]{:S(2)}, u32[]{:S(2)}) collective-permute-start(bf16[128,512]{1,0:T(8,128)(2,1)S(1)} %pad_maximum_fusion.5), channel_id=1, source_target_pairs={{0,56},{1,57},{2,58},{3,59},{4,60},{5,61},{6,62},{7,63},{8,0},{9,1... | collective-permute-start | bytes 393224 | tf_op jit(solution)/shard_map/ppermute | solution.py:296
  11.2 2.6 scatter_custom_fusion
  14.5 8.8 %all-to-all-start = ((s32[64,1,16]{2,1,0:T(1,128)}), s32[64,1,16]{2,1,0:T(1,128)S(1)}, u32[]{:S(2)}, u32[]{:S(2)}) async-start(s32[64,1,16]{2,1,0:T(1,128)} %bitcast.6), calls=%async_computation | async-start | bytes 65536 | tf_op jit(solution)/shard_map/all_to_all | solution.py:451
  28.1 4.5 %all-to-all-done = s32[64,1,16]{2,1,0:T(1,128)S(1)} async-done(((s32[64,1,16]{2,1,0:T(1,128)}), s32[64,1,16]{2,1,0:T(1,128)S(1)}, u32[]{:S(2)}, u32[]{:S(2)}) %all-to-all-start) | async-done | bytes 4128 | tf_op jit(solution)/shard_map/all_to_all | solution.py:451
  32.6 3.9 %all-to-all-start.2 = ((s32[8,1,256]{2,1,0:T(1,128)}), s32[8,1,256]{2,1,0:T(1,128)S(1)}, u32[]{:S(2)}, u32[]{:S(2)}) async-start(s32[8,1,256]{2,1,0:T(1,128)} %all_to_all.31), calls=%async_computation.2 | async-start | bytes 16384 | tf_op jit(solution)/shard_map/all_to_all | solution.py:452
  37.2 4.6 %pick.1 = bf16[1536,512]{1,0:T(8,128)(2,1)} custom-call(s32[1,1536]{1,0:T(1,128)} %reshape.111.ids_ref, bf16[1024,512]{1,0:T(8,128)(2,1)} %fusion.3.table_ref), custom_call_target="tpu_custom_call" | custom-call | flops 2147483648 | bytes 3145728 | tf_op jit(solution)/shard_map/pick/pallas_call | solution.py:373
  41.9 6.9 %all-to-all-start.1 = ((bf16[64,24,512]{2,1,0:T(8,128)(2,1)}), bf16[64,24,512]{2,1,0:T(8,128)(2,1)}, u32[]{:S(2)}, u32[]{:S(2)}) async-start(bf16[64,24,512]{2,1,0:T(8,128)(2,1)} %bitcast.42), calls=%async_computation.1 | async-start | bytes 3145728 | tf_op jit(solution)/shard_map/all_to_all | solution.py:461
  49.7 3.3 %collective-permute-start.2 = (bf16[384,512]{1,0:T(8,128)(2,1)S(1)}, bf16[384,512]{1,0:T(8,128)(2,1)S(1)}, u32[]{:S(2)}, u32[]{:S(2)}) collective-permute-start(bf16[384,512]{1,0:T(8,128)(2,1)S(1)} %pad_maximum_fusion.3.here), channel_id=1, source_target_pairs={{0,24},{1,25},{2,26},{3,27},{4,28},{5,29},{6,30},{7,31},{8,32},{9,... | collective-permute-start | bytes 1179656 | tf_op jit(solution)/shard_map/ppermute | solution.py:296
  55.8 56.8 %collective-permute-done.2.behind = bf16[384,512]{1,0:T(8,128)(2,1)S(1)} collective-permute-done((bf16[384,512]{1,0:T(8,128)(2,1)S(1)}, bf16[384,512]{1,0:T(8,128)(2,1)S(1)}, u32[]{:S(2)}, u32[]{:S(2)}) %collective-permute-start.2) | collective-permute-done | bytes 393248 | tf_op jit(solution)/shard_map/ppermute | solution.py:296
  113.4 3.3 %answer.1 = (bf16[1024,512]{1,0:T(8,128)(2,1)}, bf16[1024,512]{1,0:T(8,128)(2,1)}) custom-call(s32[1]{0:T(128)} %bitcast.14.me_ref, s32[8,256]{1,0:T(8,128)} %reshape.116.ids_ref, bf16[384,512]{1,0:T(8,128)(2,1)} %copy-done.6, bf16[384,512]{1,0:T(8,128)(2,1)} %copy-done.22, bf16[384,512]{1,0:T(8,128)(2,1)} %copy-done.23), custom_call_target="tpu_custom_call" | custom-call | flops 1073741824 | bytes 4194304 | tf_op jit(solution)/shard_map/answer/pallas_call | solution.py:208
  123.1 2.4 collective-permute-start.6
  130.8 3.8 %collective-permute-done.5.refs_2_ = bf16[512,512]{1,0:T(8,128)(2,1)} collective-permute-done((bf16[512,512]{1,0:T(8,128)(2,1)}, bf16[512,512]{1,0:T(8,128)(2,1)}, u32[]{:S(2)}, u32[]{:S(2)}) %collective-permute-start.5) | collective-permute-done | bytes 524320 | tf_op jit(solution)/shard_map/ppermute | solution.py:300
  134.5 13.4 %collective-permute-done.6.refs_3_ = bf16[512,512]{1,0:T(8,128)(2,1)} collective-permute-done((bf16[512,512]{1,0:T(8,128)(2,1)}, bf16[512,512]{1,0:T(8,128)(2,1)}, u32[]{:S(2)}, u32[]{:S(2)}) %collective-permute-start.6) | collective-permute-done | bytes 524320 | tf_op jit(solution)/shard_map/ppermute | solution.py:300
  147.9 2.8 collective-permute-done.7.refs_4_
  150.8 16.6 %edge.1 = (s16[1024,512]{1,0:T(8,128)(2,1)}, s16[1024,512]{1,0:T(8,128)(2,1)}, s16[1536,512]{1,0:T(8,128)(2,1)}) custom-call(s32[512,1]{1,0:T(8,128)} %get-tuple-element.55.slot_col, s32[1,512]{1,0:T(1,128)} %add.118.slot_row, s32[512,1]{1,0:T(8,128)} %copy.63.tail_col, s32[1,512]{1,0:T(1,128)} %bitcast.51, f32[512,512]{1,0:T(8,128)} %select_maximum_fusion.rel_ref, ...), custom_call_target="tpu_custom_call" | custom-call | flops 9663676416 | bytes 16777216 | tf_op jit(solution)/shard_map/edge/pallas_call | solution.py:163
  167.4 6.0 %all-to-all-start.3 = ((s16[64,24,512]{2,1,0:T(8,128)(2,1)}), s16[64,24,512]{2,1,0:T(8,128)(2,1)S(1)}, u32[]{:S(2)}, u32[]{:S(2)}) async-start(s16[64,24,512]{2,1,0:T(8,128)(2,1)} %bitcast.43), calls=%async_computation.3 | async-start | bytes 3145728 | tf_op jit(solution)/shard_map/all_to_all | solution.py:469
  174.1 2.4 collective-permute-done.14.refs_1_
  178.0 2.5 collective-permute-start.16
  182.0 17.7 %collective-permute-done.15.refs_2_ = s16[512,512]{1,0:T(8,128)(2,1)} collective-permute-done((s16[512,512]{1,0:T(8,128)(2,1)S(1)}, s16[512,512]{1,0:T(8,128)(2,1)}, u32[]{:S(2)}, u32[]{:S(2)}) %collective-permute-start.15) | collective-permute-done | bytes 524320 | tf_op jit(solution)/shard_map/ppermute | solution.py:300
  199.7 18.0 %collective-permute-done.16.refs_3_ = s16[512,512]{1,0:T(8,128)(2,1)} collective-permute-done((s16[512,512]{1,0:T(8,128)(2,1)S(1)}, s16[512,512]{1,0:T(8,128)(2,1)}, u32[]{:S(2)}, u32[]{:S(2)}) %collective-permute-start.16) | collective-permute-done | bytes 524320 | tf_op jit(solution)/shard_map/ppermute | solution.py:300
  218.8 7.0 %shard_map.131 = (f32[256,512]{1,0:T(8,128)}, s16[256,512]{1,0:T(8,128)(2,1)}, s16[256,512]{1,0:T(8,128)(2,1)}, s16[256,512]{1,0:T(8,128)(2,1)}) custom-call(s32[1]{0:T(128)} %bitcast.me_ref, s32[8,256]{1,0:T(8,128)} %reshape.116.ids_ref, s16[1024,512]{1,0:T(8,128)(2,1)} %get-tuple-element.29.refs_0_, s16[1024,512]{1,0:T(8,128)(2,1)} %copy-done.5, ...), custom_call_target="tpu_custom_call" | custom-call | flops 4294967296 | bytes 8388608 | tf_op jit(solution)/shard_map/pallas_call | solution.py:280
  227.1 2.4 collective-permute-start.19
  231.8 6.8 %shard_map.129 = (f32[256,512]{1,0:T(8,128)}, s16[256,512]{1,0:T(8,128)(2,1)}, s16[256,512]{1,0:T(8,128)(2,1)}, s16[256,512]{1,0:T(8,128)(2,1)}) custom-call(s32[1]{0:T(128)} %bitcast.me_ref, s32[1,1536]{1,0:T(1,128)} %reshape.110.ids_ref, s32[1,8]{1,0:T(1,128)} %neg_ref.1, s16[64,24,512]{2,1,0:T(8,128)(2,1)} %copy-done.1), custom_call_target="tpu_custom_call" | custom-call | flops 4294967296 | bytes 8388608 | tf_op jit(solution)/shard_map/pallas_call | solution.py:280
  244.2 6.7 %all-to-all-start.4 = ((f32[8,32,512]{2,1,0:T(8,128)}), f32[8,32,512]{2,1,0:T(8,128)S(1)}, u32[]{:S(2)}, u32[]{:S(2)}) async-start(f32[8,32,512]{2,1,0:T(8,128)} %bitcast.41), calls=%async_computation.4 | async-start | bytes 1048576 | tf_op jit(solution)/shard_map/all_to_all | solution.py:495
  252.0 2.8 collective-permute-start.9
  254.8 3.1 %collective-permute-done.8.refs_0_ = s16[256,512]{1,0:T(8,128)(2,1)S(1)} collective-permute-done((s16[256,512]{1,0:T(8,128)(2,1)S(1)}, s16[256,512]{1,0:T(8,128)(2,1)S(1)}, u32[]{:S(2)}, u32[]{:S(2)}) %collective-permute-start.8) | collective-permute-done | bytes 262176 | tf_op jit(solution)/shard_map/ppermute | solution.py:292
  257.9 8.1 %collective-permute-done.9.refs_1_ = s16[256,512]{1,0:T(8,128)(2,1)S(1)} collective-permute-done((s16[256,512]{1,0:T(8,128)(2,1)S(1)}, s16[256,512]{1,0:T(8,128)(2,1)S(1)}, u32[]{:S(2)}, u32[]{:S(2)}) %collective-permute-start.9) | collective-permute-done | bytes 262176 | tf_op jit(solution)/shard_map/ppermute | solution.py:292
  270.0 2.9 collective-permute-start.12
  272.9 4.6 %collective-permute-done.11.refs_1_ = s16[256,512]{1,0:T(8,128)(2,1)S(1)} collective-permute-done((s16[256,512]{1,0:T(8,128)(2,1)}, s16[256,512]{1,0:T(8,128)(2,1)S(1)}, u32[]{:S(2)}, u32[]{:S(2)}) %collective-permute-start.11) | collective-permute-done | bytes 262176 | tf_op jit(solution)/shard_map/ppermute | solution.py:292
  277.5 6.7 %collective-permute-done.12.refs_2_ = s16[256,512]{1,0:T(8,128)(2,1)S(1)} collective-permute-done((s16[256,512]{1,0:T(8,128)(2,1)}, s16[256,512]{1,0:T(8,128)(2,1)S(1)}, u32[]{:S(2)}, u32[]{:S(2)}) %collective-permute-start.12) | collective-permute-done | bytes 262176 | tf_op jit(solution)/shard_map/ppermute | solution.py:292
  285.4 3.8 %update.1 = (f32[400,1024]{1,0:T(8,128)}, f32[1,1024]{1,0:T(1,128)}) custom-call(s32[1]{0:T(128)} %bitcast.me_ref, f32[400,1024]{1,0:T(8,128)} %bitcast.40, f32[1,1024]{1,0:T(1,128)} %bitcast.52, s16[256,512]{1,0:T(8,128)(2,1)} %shard_map.130.refs_0_, s16[256,512]{1,0:T(8,128)(2,1)} %copy-done.7, s16[256,512]{1,0:T(8,128)(2,1)} %copy-done.8, ...), custom_call_target="tpu_custom_call" | custom-call | tf_op jit(solution)/shard_map/update/pallas_call | solution.py:347
  290.1 3.7 %collective-permute-start.22 = (f32[32,512]{1,0:T(8,128)S(1)}, f32[32,512]{1,0:T(8,128)S(1)}, u32[]{:S(2)}, u32[]{:S(2)}) collective-permute-start(f32[32,512]{1,0:T(8,128)S(1)} %reduce_sum.48), channel_id=1, source_target_pairs={{0,128},{64,192},{128,0},{192,64},{1,129},{65,193},{129,1},{193,65... | collective-permute-start | bytes 196616 | tf_op jit(solution)/shard_map/ppermute | solution.py:292
  (159 shorter events, 52.5 us)
Async XLA Ops:
  0.6 22.7 %copy-start = (f32[1024,400]{0,1:T(8,128)S(1)}, f32[1024,400]{0,1:T(8,128)}, u32[]{:S(2)}) copy-start(f32[1024,400]{0,1:T(8,128)} %param.10) | copy-start | bytes 4915204
  2.7 46.1 %collective-permute-start.1 = (bf16[128,512]{1,0:T(8,128)(2,1)S(1)}, bf16[128,512]{1,0:T(8,128)(2,1)S(1)}, u32[]{:S(2)}, u32[]{:S(2)}) collective-permute-start(bf16[128,512]{1,0:T(8,128)(2,1)S(1)} %pad_maximum_fusion.5), channel_id=1, source_target_pairs={{0,56},{1,57},{2,58},{3,59},{4,60},{5,61},{6,62},{7,63},{8,0},{9,1... | collective-permute-start | bytes 393224 | tf_op jit(solution)/shard_map/ppermute | solution.py:296
  9.1 39.6 %collective-permute-start = (bf16[128,512]{1,0:T(8,128)(2,1)S(1)}, bf16[128,512]{1,0:T(8,128)(2,1)}, u32[]{:S(2)}, u32[]{:S(2)}) collective-permute-start(bf16[128,512]{1,0:T(8,128)(2,1)S(1)} %pad_maximum_fusion.5), channel_id=1, source_target_pairs={{0,8},{1,9},{2,10},{3,11},{4,12},{5,13},{6,14},{7,15},{8,16},{9,17... | collective-permute-start | bytes 393224 | tf_op jit(solution)/shard_map/ppermute | solution.py:296
  14.5 18.1 %all-to-all-start = ((s32[64,1,16]{2,1,0:T(1,128)}), s32[64,1,16]{2,1,0:T(1,128)S(1)}, u32[]{:S(2)}, u32[]{:S(2)}) async-start(s32[64,1,16]{2,1,0:T(1,128)} %bitcast.6), calls=%async_computation | async-start | bytes 65536 | tf_op jit(solution)/shard_map/all_to_all | solution.py:451
  32.6 9.2 %all-to-all-start.2 = ((s32[8,1,256]{2,1,0:T(1,128)}), s32[8,1,256]{2,1,0:T(1,128)S(1)}, u32[]{:S(2)}, u32[]{:S(2)}) async-start(s32[8,1,256]{2,1,0:T(1,128)} %all_to_all.31), calls=%async_computation.2 | async-start | bytes 16384 | tf_op jit(solution)/shard_map/all_to_all | solution.py:452
  41.9 108.9 %all-to-all-start.1 = ((bf16[64,24,512]{2,1,0:T(8,128)(2,1)}), bf16[64,24,512]{2,1,0:T(8,128)(2,1)}, u32[]{:S(2)}, u32[]{:S(2)}) async-start(bf16[64,24,512]{2,1,0:T(8,128)(2,1)} %bitcast.42), calls=%async_computation.1 | async-start | bytes 3145728 | tf_op jit(solution)/shard_map/all_to_all | solution.py:461
  49.7 62.8 %copy-start.6 = (bf16[384,512]{1,0:T(8,128)(2,1)}, bf16[384,512]{1,0:T(8,128)(2,1)S(1)}, u32[]{:S(2)}) copy-start(bf16[384,512]{1,0:T(8,128)(2,1)S(1)} %pad_maximum_fusion.3.here) | copy-start | bytes 1179652
  49.7 62.8 %collective-permute-start.2 = (bf16[384,512]{1,0:T(8,128)(2,1)S(1)}, bf16[384,512]{1,0:T(8,128)(2,1)S(1)}, u32[]{:S(2)}, u32[]{:S(2)}) collective-permute-start(bf16[384,512]{1,0:T(8,128)(2,1)S(1)} %pad_maximum_fusion.3.here), channel_id=1, source_target_pairs={{0,24},{1,25},{2,26},{3,27},{4,28},{5,29},{6,30},{7,31},{8,32},{9,... | collective-permute-start | bytes 1179656 | tf_op jit(solution)/shard_map/ppermute | solution.py:296
  53.0 59.5 %collective-permute-start.3 = (bf16[384,512]{1,0:T(8,128)(2,1)S(1)}, bf16[384,512]{1,0:T(8,128)(2,1)S(1)}, u32[]{:S(2)}, u32[]{:S(2)}) collective-permute-start(bf16[384,512]{1,0:T(8,128)(2,1)S(1)} %pad_maximum_fusion.3.here), channel_id=1, source_target_pairs={{0,40},{1,41},{2,42},{3,43},{4,44},{5,45},{6,46},{7,47},{8,48},{9,... | collective-permute-start | bytes 1179656 | tf_op jit(solution)/shard_map/ppermute | solution.py:296
  116.7 3.5 %collective-permute-start.4 = (bf16[1024,512]{1,0:T(8,128)(2,1)}, bf16[1024,512]{1,0:T(8,128)(2,1)S(1)}, u32[]{:S(2)}, u32[]{:S(2)}) collective-permute-start(bf16[1024,512]{1,0:T(8,128)(2,1)} %get-tuple-element.21), channel_id=1, source_target_pairs={{0,1},{1,0},{2,3},{3,2},{4,5},{5,4},{6,7},{7,6},{8,9},{9,8},{10,11... | collective-permute-start | bytes 3145736 | tf_op jit(solution)/shard_map/ppermute | solution.py:300
  121.1 13.4 %collective-permute-start.5 = (bf16[512,512]{1,0:T(8,128)(2,1)}, bf16[512,512]{1,0:T(8,128)(2,1)}, u32[]{:S(2)}, u32[]{:S(2)}) collective-permute-start(bf16[512,512]{1,0:T(8,128)(2,1)} %pad_maximum_fusion), channel_id=1, source_target_pairs={{0,2},{1,3},{2,0},{3,1},{4,6},{5,7},{6,4},{7,5},{8,10},{9,11},{10,... | collective-permute-start | bytes 1572872 | tf_op jit(solution)/shard_map/ppermute | solution.py:300
  123.1 24.8 %collective-permute-start.6 = (bf16[512,512]{1,0:T(8,128)(2,1)}, bf16[512,512]{1,0:T(8,128)(2,1)}, u32[]{:S(2)}, u32[]{:S(2)}) collective-permute-start(bf16[512,512]{1,0:T(8,128)(2,1)} %pad_maximum_fusion.1), channel_id=1, source_target_pairs={{0,4},{1,5},{2,6},{3,7},{4,0},{5,1},{6,2},{7,3},{8,12},{9,13},{10,... | collective-permute-start | bytes 1572872 | tf_op jit(solution)/shard_map/ppermute | solution.py:300
  125.6 25.2 %collective-permute-start.7 = (bf16[512,512]{1,0:T(8,128)(2,1)S(1)}, bf16[512,512]{1,0:T(8,128)(2,1)}, u32[]{:S(2)}, u32[]{:S(2)}) collective-permute-start(bf16[512,512]{1,0:T(8,128)(2,1)S(1)} %pad_maximum_fusion.2), channel_id=1, source_target_pairs={{0,6},{1,7},{2,4},{3,5},{4,2},{5,3},{6,0},{7,1},{8,14},{9,15},{10,... | collective-permute-start | bytes 1572872 | tf_op jit(solution)/shard_map/ppermute | solution.py:300
  167.4 63.3 %all-to-all-start.3 = ((s16[64,24,512]{2,1,0:T(8,128)(2,1)}), s16[64,24,512]{2,1,0:T(8,128)(2,1)S(1)}, u32[]{:S(2)}, u32[]{:S(2)}) async-start(s16[64,24,512]{2,1,0:T(8,128)(2,1)} %bitcast.43), calls=%async_computation.3 | async-start | bytes 3145728 | tf_op jit(solution)/shard_map/all_to_all | solution.py:469
  173.4 3.2 %collective-permute-start.14 = (s16[1024,512]{1,0:T(8,128)(2,1)}, s16[1024,512]{1,0:T(8,128)(2,1)S(1)}, u32[]{:S(2)}, u32[]{:S(2)}) collective-permute-start(s16[1024,512]{1,0:T(8,128)(2,1)} %get-tuple-element.30), channel_id=1, source_target_pairs={{0,1},{1,0},{2,3},{3,2},{4,5},{5,4},{6,7},{7,6},{8,9},{9,8},{10,11... | collective-permute-start | bytes 3145736 | tf_op jit(solution)/shard_map/ppermute | solution.py:300
  176.7 23.0 %collective-permute-start.15 = (s16[512,512]{1,0:T(8,128)(2,1)S(1)}, s16[512,512]{1,0:T(8,128)(2,1)}, u32[]{:S(2)}, u32[]{:S(2)}) collective-permute-start(s16[512,512]{1,0:T(8,128)(2,1)S(1)} %pad_add_fusion), channel_id=1, source_target_pairs={{0,2},{1,3},{2,0},{3,1},{4,6},{5,7},{6,4},{7,5},{8,10},{9,11},{10,... | collective-permute-start | bytes 1572872 | tf_op jit(solution)/shard_map/ppermute | solution.py:300
  178.0 39.7 %collective-permute-start.16 = (s16[512,512]{1,0:T(8,128)(2,1)S(1)}, s16[512,512]{1,0:T(8,128)(2,1)}, u32[]{:S(2)}, u32[]{:S(2)}) collective-permute-start(s16[512,512]{1,0:T(8,128)(2,1)S(1)} %pad_add_fusion.1), channel_id=1, source_target_pairs={{0,4},{1,5},{2,6},{3,7},{4,0},{5,1},{6,2},{7,3},{8,12},{9,13},{10,... | collective-permute-start | bytes 1572872 | tf_op jit(solution)/shard_map/ppermute | solution.py:300
  180.5 38.3 %collective-permute-start.17 = (s16[512,512]{1,0:T(8,128)(2,1)S(1)}, s16[512,512]{1,0:T(8,128)(2,1)}, u32[]{:S(2)}, u32[]{:S(2)}) collective-permute-start(s16[512,512]{1,0:T(8,128)(2,1)S(1)} %pad_add_fusion.2), channel_id=1, source_target_pairs={{0,6},{1,7},{2,4},{3,5},{4,2},{5,3},{6,0},{7,1},{8,14},{9,15},{10,... | collective-permute-start | bytes 1572872 | tf_op jit(solution)/shard_map/ppermute | solution.py:300
  225.9 12.8 %collective-permute-start.18 = (s16[256,512]{1,0:T(8,128)(2,1)}, s16[256,512]{1,0:T(8,128)(2,1)S(1)}, u32[]{:S(2)}, u32[]{:S(2)}) collective-permute-start(s16[256,512]{1,0:T(8,128)(2,1)} %get-tuple-element.33), channel_id=1, source_target_pairs={{0,64},{64,128},{128,192},{192,0},{1,65},{65,129},{129,193},{193,1... | collective-permute-start | bytes 786440 | tf_op jit(solution)/shard_map/ppermute | solution.py:292
  227.1 13.4 %collective-permute-start.19 = (s16[256,512]{1,0:T(8,128)(2,1)}, s16[256,512]{1,0:T(8,128)(2,1)S(1)}, u32[]{:S(2)}, u32[]{:S(2)}) collective-permute-start(s16[256,512]{1,0:T(8,128)(2,1)} %get-tuple-element.34), channel_id=1, source_target_pairs={{0,128},{64,192},{128,0},{192,64},{1,129},{65,193},{129,1},{193,65... | collective-permute-start | bytes 786440 | tf_op jit(solution)/shard_map/ppermute | solution.py:292
  229.5 11.1 %collective-permute-start.20 = (s16[256,512]{1,0:T(8,128)(2,1)}, s16[256,512]{1,0:T(8,128)(2,1)S(1)}, u32[]{:S(2)}, u32[]{:S(2)}) collective-permute-start(s16[256,512]{1,0:T(8,128)(2,1)} %get-tuple-element.35), channel_id=1, source_target_pairs={{0,192},{64,0},{128,64},{192,128},{1,193},{65,1},{129,65},{193,129... | collective-permute-start | bytes 786440 | tf_op jit(solution)/shard_map/ppermute | solution.py:292
  238.7 16.1 %copy-start.24 = (s16[256,512]{1,0:T(8,128)(2,1)S(1)}, s16[256,512]{1,0:T(8,128)(2,1)}, u32[]{:S(2)}) copy-start(s16[256,512]{1,0:T(8,128)(2,1)} %get-tuple-element.26) | copy-start | bytes 786436
  244.2 45.0 %all-to-all-start.4 = ((f32[8,32,512]{2,1,0:T(8,128)}), f32[8,32,512]{2,1,0:T(8,128)S(1)}, u32[]{:S(2)}, u32[]{:S(2)}) async-start(f32[8,32,512]{2,1,0:T(8,128)} %bitcast.41), calls=%async_computation.4 | async-start | bytes 1048576 | tf_op jit(solution)/shard_map/all_to_all | solution.py:495
  250.9 7.0 %collective-permute-start.8 = (s16[256,512]{1,0:T(8,128)(2,1)S(1)}, s16[256,512]{1,0:T(8,128)(2,1)S(1)}, u32[]{:S(2)}, u32[]{:S(2)}) collective-permute-start(s16[256,512]{1,0:T(8,128)(2,1)S(1)} %copy-done.26), channel_id=1, source_target_pairs={{0,64},{64,128},{128,192},{192,0},{1,65},{65,129},{129,193},{193,1... | collective-permute-start | bytes 786440 | tf_op jit(solution)/shard_map/ppermute | solution.py:292
  252.0 14.0 %collective-permute-start.9 = (s16[256,512]{1,0:T(8,128)(2,1)S(1)}, s16[256,512]{1,0:T(8,128)(2,1)S(1)}, u32[]{:S(2)}, u32[]{:S(2)}) collective-permute-start(s16[256,512]{1,0:T(8,128)(2,1)S(1)} %copy-done.25), channel_id=1, source_target_pairs={{0,128},{64,192},{128,0},{192,64},{1,129},{65,193},{129,1},{193,65... | collective-permute-start | bytes 786440 | tf_op jit(solution)/shard_map/ppermute | solution.py:292
  254.8 11.2 %collective-permute-start.10 = (s16[256,512]{1,0:T(8,128)(2,1)S(1)}, s16[256,512]{1,0:T(8,128)(2,1)S(1)}, u32[]{:S(2)}, u32[]{:S(2)}) collective-permute-start(s16[256,512]{1,0:T(8,128)(2,1)S(1)} %copy-done.24), channel_id=1, source_target_pairs={{0,192},{64,0},{128,64},{192,128},{1,193},{65,1},{129,65},{193,129... | collective-permute-start | bytes 786440 | tf_op jit(solution)/shard_map/ppermute | solution.py:292
  269.8 7.7 %collective-permute-start.11 = (s16[256,512]{1,0:T(8,128)(2,1)}, s16[256,512]{1,0:T(8,128)(2,1)S(1)}, u32[]{:S(2)}, u32[]{:S(2)}) collective-permute-start(s16[256,512]{1,0:T(8,128)(2,1)} %shard_map.130.refs_0_), channel_id=1, source_target_pairs={{0,64},{64,128},{128,192},{192,0},{1,65},{65,129},{129,193},{193,1... | collective-permute-start | bytes 786440 | tf_op jit(solution)/shard_map/ppermute | solution.py:292
  270.0 14.2 %collective-permute-start.12 = (s16[256,512]{1,0:T(8,128)(2,1)}, s16[256,512]{1,0:T(8,128)(2,1)S(1)}, u32[]{:S(2)}, u32[]{:S(2)}) collective-permute-start(s16[256,512]{1,0:T(8,128)(2,1)} %shard_map.130.refs_0_), channel_id=1, source_target_pairs={{0,128},{64,192},{128,0},{192,64},{1,129},{65,193},{129,1},{193,65... | collective-permute-start | bytes 786440 | tf_op jit(solution)/shard_map/ppermute | solution.py:292
  272.9 11.8 %collective-permute-start.13 = (s16[256,512]{1,0:T(8,128)(2,1)}, s16[256,512]{1,0:T(8,128)(2,1)S(1)}, u32[]{:S(2)}, u32[]{:S(2)}) collective-permute-start(s16[256,512]{1,0:T(8,128)(2,1)} %shard_map.130.refs_0_), channel_id=1, source_target_pairs={{0,192},{64,0},{128,64},{192,128},{1,193},{65,1},{129,65},{193,129... | collective-permute-start | bytes 786440 | tf_op jit(solution)/shard_map/ppermute | solution.py:292
  289.3 5.0 %collective-permute-start.21 = (f32[32,512]{1,0:T(8,128)S(1)}, f32[32,512]{1,0:T(8,128)S(1)}, u32[]{:S(2)}, u32[]{:S(2)}) collective-permute-start(f32[32,512]{1,0:T(8,128)S(1)} %reduce_sum.48), channel_id=1, source_target_pairs={{0,64},{64,128},{128,192},{192,0},{1,65},{65,129},{129,193},{193,1... | collective-permute-start | bytes 196616 | tf_op jit(solution)/shard_map/ppermute | solution.py:292
  290.1 6.5 %collective-permute-start.22 = (f32[32,512]{1,0:T(8,128)S(1)}, f32[32,512]{1,0:T(8,128)S(1)}, u32[]{:S(2)}, u32[]{:S(2)}) collective-permute-start(f32[32,512]{1,0:T(8,128)S(1)} %reduce_sum.48), channel_id=1, source_target_pairs={{0,128},{64,192},{128,0},{192,64},{1,129},{65,193},{129,1},{193,65... | collective-permute-start | bytes 196616 | tf_op jit(solution)/shard_map/ppermute | solution.py:292
  293.8 3.6 %collective-permute-start.23 = (f32[32,512]{1,0:T(8,128)S(1)}, f32[32,512]{1,0:T(8,128)S(1)}, u32[]{:S(2)}, u32[]{:S(2)}) collective-permute-start(f32[32,512]{1,0:T(8,128)S(1)} %reduce_sum.48), channel_id=1, source_target_pairs={{0,192},{64,0},{128,64},{192,128},{1,193},{65,1},{129,65},{193,129... | collective-permute-start | bytes 196616 | tf_op jit(solution)/shard_map/ppermute | solution.py:292
  (25 other events, 103.5 us)
where the time goes:
time: 300 us; the launch traced here: 299 us
  waiting for transfers between devices  150 us (50%)
  starting transfers between devices  69.9 us (23%)
  Pallas kernels  46.8 us (16%)
  local copies, waits for them, and re-layouts  20.9 us (7%)
  other arithmetic  9.33 us (3%)
    ppermute x8, waiting for transfers between devices, near_swap(): return lax.ppermute(x, 'table', [(i, i ^ other) for i in range(n_table)])  60.3 us
    ppermute x4, waiting for transfers between devices, ring_shift(): lax.ppermute(x, 'table', [(i, (i + step * GROUP) % n_table) for i in rang...  56.8 us
    ppermute x12, waiting for transfers between devices, shift(): lax.ppermute(x, 'rep', [(i, (i + step) % n_rep) for i in range(n_rep)])  28.5 us
    pallas_call x1, Pallas kernels, edge_call(): pl.pallas_call(edge_kernel, in_specs=[vmem()] * (6 + len(pieces)), out_sp...  16.6 us
    ppermute x12, starting transfers between devices, shift(): lax.ppermute(x, 'rep', [(i, (i + step) % n_rep) for i in range(n_rep)])  16.4 us
    pallas_call x2, Pallas kernels, parts_call(): pl.pallas_call(functools.partial(kernel, n_rep=n_rep), in_specs=[smem()]...  13.9 us
    ppermute x4, starting transfers between devices, ring_shift(): lax.ppermute(x, 'table', [(i, (i + step * GROUP) % n_table) for i in rang...  11.2 us
    ppermute x8, starting transfers between devices, near_swap(): return lax.ppermute(x, 'table', [(i, i ^ other) for i in range(n_table)])  10.1 us
  transfers between devices with their start and end apart: 29, of which 20 were waited for; matrix products, arithmetic and copies ran while one was open for 7% of the time, Pallas kernels for 9%

commit v1 on v0

--- a/solution.py
+++ b/solution.py
@@ -68,6 +68,29 @@
     lane = lax.broadcasted_iota(I32, x.shape, x.ndim - 1)
     scale = jnp.exp2(x[..., FULL - 1 :] - 14.0)
     return jnp.where(lane >= FULL - 8, 0.0, x * scale)
+
+
+POWER_ROWS = 16
+
+
+def across(x, width):
+    half = width // 2
+    x = x.T
+    return jnp.concatenate([x[:half], x[HALF : HALF + half]], axis=0)
+
+
+def packed_across(x):
+    peak = jnp.max(jnp.abs(x), axis=0, keepdims=True)
+    power = jnp.floor(jnp.log(jnp.maximum(peak, 1e-30)) * 1.4426950408889634)
+    code = jnp.clip(jnp.round(x * jnp.exp2(14.0 - power)), -32767.0, 32767.0)
+    power = jnp.broadcast_to(power, (POWER_ROWS, x.shape[1]))
+    return jnp.concatenate([code, power], axis=0).astype(I32).astype(I16)
+
+
+def unpacked_across(code):
+    x = code.astype(F32)
+    width = x.shape[0] - POWER_ROWS
+    return x[:width] * jnp.exp2(x[width : width + 1] - 14.0)
 
 
 def with_rel(rel, v):
@@ -218,9 +241,9 @@
 def coded_parts(src, own_ref, msgs, me, n_rep):
     @pl.loop(0, n_rep)
     def _(k):
-        part = src(lax.rem(me + k, n_rep))
+        part = across(src(lax.rem(me + k, n_rep)), own_ref.shape[0])
         pl.when(k == 0)(functools.partial(put, own_ref, part))
-        code = packed(part)
+        code = packed_across(part)
         for step in range(1, n_rep):
             pl.when(k == step)(functools.partial(put, msgs[step - 1], code))
 
@@ -252,7 +275,7 @@
 def cold_kernel(me_ref, ids_ref, neg_ref, back_ref, own_ref, *refs, n_rep):
     n_src, per, _ = back_ref.shape
     msgs, flat = refs[:-1], refs[-1]
-    quarter = own_ref.shape[0]
+    quarter = own_ref.shape[1]
     back = unpacked(back_ref[...])
     negs = per - HEAD_CAP
     neg_sum = jnp.sum(back[:, HEAD_CAP:, :], axis=0)
@@ -276,13 +299,13 @@
     return pl.BlockSpec(memory_space=pltpu.VMEM)
 
 
-def parts_call(kernel, me, operands, rows, scratch, n_rep):
+def parts_call(kernel, me, operands, width, rows, scratch, n_rep):
     return pl.pallas_call(
         functools.partial(kernel, n_rep=n_rep),
         in_specs=[smem()] + [vmem()] * len(operands),
         out_specs=[vmem()] * n_rep,
-        out_shape=[jax.ShapeDtypeStruct((rows, FULL), F32)]
-        + [jax.ShapeDtypeStruct((rows, FULL), I16)] * (n_rep - 1),
+        out_shape=[jax.ShapeDtypeStruct((width, rows), F32)]
+        + [jax.ShapeDtypeStruct((width + POWER_ROWS, rows), I16)] * (n_rep - 1),
         scratch_shapes=[scratch],
         cost_estimate=pl.CostEstimate(flops=4 << 30, bytes_accessed=8 << 20, transcendentals=0),
     )(me, *operands)
@@ -314,30 +337,34 @@
     got, out_ref = refs[:-1], refs[-1]
     total = own_ref[...]
     for part in got:
-        total = total + unpacked(part[...])
-    out_ref[...] = packed(total) if out_ref.dtype == I16 else total
-
-
-def sum_call(own, got, dtype):
+        total = total + unpacked_across(part[...])
+    if out_ref.dtype == I16:
+        out_ref[...] = packed_across(total)
+    else:
+        half = total.shape[0] // 2
+        pad = jnp.zeros((HALF - half, total.shape[1]), F32)
+        out_ref[...] = jnp.concatenate([total[:half], pad, total[half:], pad], axis=0).T
+
+
+def sum_call(own, got, shape, dtype):
     return pl.pallas_call(
         sum_kernel,
         in_specs=[vmem()] * (1 + len(got)),
         out_specs=vmem(),
-        out_shape=jax.ShapeDtypeStruct(own.shape, dtype),
+        out_shape=jax.ShapeDtypeStruct(shape, dtype),
     )(own, *got)
 
 
 def update_kernel(me_ref, table_ref, state_ref, *refs):
     parts, table_out, state_out = refs[:-2], refs[-2], refs[-1]
     n_rep = len(parts)
-    half = table_ref.shape[0] // 2
+    width = table_ref.shape[0]
     for k in range(n_rep):
-        quarter = parts[k].shape[0]
+        quarter = parts[k].shape[1]
         q = lax.rem(me_ref[0] - k + n_rep, n_rep)
         at = pl.ds(pl.multiple_of(q * quarter, quarter), quarter)
-        grad = unpacked(parts[k][...]).T
-        grad = jnp.concatenate([grad[:half], grad[HALF : HALF + half]], axis=0)
-        state = state_ref[:, at] + jnp.sum(grad * grad, axis=0, keepdims=True) / (2 * half)
+        grad = unpacked_across(parts[k][...])
+        state = state_ref[:, at] + jnp.sum(grad * grad, axis=0, keepdims=True) / width
         state_out[:, at] = state
         table_out[:, at] = table_ref[:, at] - learn_rate * grad / jnp.sqrt(state)
 
@@ -429,6 +456,7 @@
     rank = jnp.sum(before * owner_hot.astype(F32), axis=1).astype(jnp.int32)
     head_slot = head_owner[:, 0] * per + rank
 
+    edge_tail, _ = lax.optimization_barrier((edge_tail, here))
     block = edge_tail // hot_rows
     within = edge_tail % hot_rows
     block_hot = one_hot(block, n_table)
@@ -474,6 +502,7 @@
         dense_kernel,
         me,
         (dense_ids, *tail_got),
+        width,
         n_ring * quarter,
         pltpu.VMEM((n_ring, hot_rows, FULL), F32),
         n_rep,
@@ -483,6 +512,7 @@
         cold_kernel,
         me,
         (head_ids.reshape(1, n_table * per), neg_ids, back),
+        width,
         cold_rows // n_rep,
         pltpu.VMEM((n_table * per, FULL), BF),
         n_rep,
@@ -491,11 +521,11 @@
     for k in range(1, n_rep):
         cold_got.append(shift(cold_msg[k - 1], k, n_rep))
     hot_own, _ = lax.optimization_barrier((hot_own, cold_own))
-    hot_part = sum_call(hot_own, hot_got, F32)
+    hot_part = sum_call(hot_own, hot_got, (n_ring * quarter, FULL), F32)
     hot_rows_got = lax.all_to_all(
         hot_part.reshape(n_ring, quarter, FULL), "table", 0, 0, axis_index_groups=far
     )
-    cold_part = sum_call(cold_own, cold_got, I16)
+    cold_part = sum_call(cold_own, cold_got, cold_got[0].shape, I16)
     cold_parts = [cold_part] + [shift(cold_part, k, n_rep) for k in range(1, n_rep)]
     hot_sum = jnp.sum(hot_rows_got, axis=0)
     new_cold_table, new_cold_state = cold_update(me, cold_table, cold_state, cold_parts)

time: 300 us -> 294 us (0.980)
    ppermute x12, waiting for transfers between devices: 28.5 us -> 21.4 us  [shift(): lax.ppermute(x, 'rep', [(i, (i + step) % n_rep) for i in range(n_rep)])]
  transfers between devices with their start and end apart: 29 -> 29, of which waited for: 20 -> 18; matrix products, arithmetic and copies ran while one was open for 7% -> 6% of each run, Pallas kernels for 9% -> 9%
where the time goes in v1:
time: 294 us
  waiting for transfers between devices  148 us (50%)
  starting transfers between devices  68.8 us (23%)
  Pallas kernels  46.4 us (16%)
  local copies, waits for them, and re-layouts  20.6 us (7%)
  other arithmetic  7.74 us (3%)
    ppermute x8, waiting for transfers between devices, near_swap(): return lax.ppermute(x, 'table', [(i, i ^ other) for i in range(n_table)])  61.5 us
    ppermute x4, waiting for transfers between devices, ring_shift(): lax.ppermute(x, 'table', [(i, (i + step * GROUP) % n_table) for i in rang...  57.7 us
    ppermute x12, waiting for transfers between devices, shift(): lax.ppermute(x, 'rep', [(i, (i + step) % n_rep) for i in range(n_rep)])  21.4 us
    pallas_call x1, Pallas kernels, edge_call(): pl.pallas_call(edge_kernel, in_specs=[vmem()] * (6 + len(pieces)), out_sp...  16.6 us
    ppermute x12, starting transfers between devices, shift(): lax.ppermute(x, 'rep', [(i, (i + step) % n_rep) for i in range(n_rep)])  16.3 us
    pallas_call x2, Pallas kernels, parts_call(): pl.pallas_call(functools.partial(kernel, n_rep=n_rep), in_specs=[smem()]...  14 us
    ppermute x4, starting transfers between devices, ring_shift(): lax.ppermute(x, 'table', [(i, (i + step * GROUP) % n_table) for i in rang...  11.2 us
    ppermute x8, starting transfers between devices, near_swap(): return lax.ppermute(x, 'table', [(i, i ^ other) for i in range(n_table)])  10.4 us
  transfers between devices with their start and end apart: 29, of which 18 were waited for; matrix products, arithmetic and copies ran while one was open for 6% of the time, Pallas kernels for 9%

profile of v1, /device:TPU:1, one launch (start us, length us, event | category | flops | bytes accessed | tf_op | source)
XLA Modules:
  0.0 293.7 jit_solution(17528221296208235331)
XLA Ops:
  2.7 6.5 %collective-permute-start.1 = (bf16[128,512]{1,0:T(8,128)(2,1)S(1)}, bf16[128,512]{1,0:T(8,128)(2,1)S(1)}, u32[]{:S(2)}, u32[]{:S(2)}) collective-permute-start(bf16[128,512]{1,0:T(8,128)(2,1)S(1)} %pad_maximum_fusion.5), channel_id=1, source_target_pairs={{0,56},{1,57},{2,58},{3,59},{4,60},{5,61},{6,62},{7,63},{8,0},{9,1... | collective-permute-start | bytes 393224 | tf_op jit(solution)/shard_map/ppermute | solution.py:319
  11.2 2.6 scatter_custom_fusion
  14.5 8.8 %all-to-all-start = ((s32[64,1,16]{2,1,0:T(1,128)}), s32[64,1,16]{2,1,0:T(1,128)S(1)}, u32[]{:S(2)}, u32[]{:S(2)}) async-start(s32[64,1,16]{2,1,0:T(1,128)} %bitcast.6), calls=%async_computation | async-start | bytes 65536 | tf_op jit(solution)/shard_map/all_to_all | solution.py:479
  25.4 7.2 %all-to-all-done = s32[64,1,16]{2,1,0:T(1,128)S(1)} async-done(((s32[64,1,16]{2,1,0:T(1,128)}), s32[64,1,16]{2,1,0:T(1,128)S(1)}, u32[]{:S(2)}, u32[]{:S(2)}) %all-to-all-start) | async-done | bytes 4128 | tf_op jit(solution)/shard_map/all_to_all | solution.py:479
  36.7 3.9 %all-to-all-start.2 = ((s32[8,1,256]{2,1,0:T(1,128)}), s32[8,1,256]{2,1,0:T(1,128)S(1)}, u32[]{:S(2)}, u32[]{:S(2)}) async-start(s32[8,1,256]{2,1,0:T(1,128)} %all_to_all.31), calls=%async_computation.2 | async-start | bytes 16384 | tf_op jit(solution)/shard_map/all_to_all | solution.py:480
  40.6 4.6 %pick.1 = bf16[1536,512]{1,0:T(8,128)(2,1)} custom-call(s32[1,1536]{1,0:T(1,128)} %reshape.111.ids_ref, bf16[1024,512]{1,0:T(8,128)(2,1)} %fusion.3.table_ref), custom_call_target="tpu_custom_call" | custom-call | flops 2147483648 | bytes 3145728 | tf_op jit(solution)/shard_map/pick/pallas_call | solution.py:400
  45.2 5.7 %all-to-all-start.1 = ((bf16[64,24,512]{2,1,0:T(8,128)(2,1)}), bf16[64,24,512]{2,1,0:T(8,128)(2,1)}, u32[]{:S(2)}, u32[]{:S(2)}) async-start(bf16[64,24,512]{2,1,0:T(8,128)(2,1)} %bitcast.42), calls=%async_computation.1 | async-start | bytes 3145728 | tf_op jit(solution)/shard_map/all_to_all | solution.py:489
  51.0 3.3 %collective-permute-start.2 = (bf16[384,512]{1,0:T(8,128)(2,1)S(1)}, bf16[384,512]{1,0:T(8,128)(2,1)S(1)}, u32[]{:S(2)}, u32[]{:S(2)}) collective-permute-start(bf16[384,512]{1,0:T(8,128)(2,1)S(1)} %pad_maximum_fusion.3.here), channel_id=1, source_target_pairs={{0,24},{1,25},{2,26},{3,27},{4,28},{5,29},{6,30},{7,31},{8,32},{9,... | collective-permute-start | bytes 1179656 | tf_op jit(solution)/shard_map/ppermute | solution.py:319
  57.0 57.7 %collective-permute-done.2.behind = bf16[384,512]{1,0:T(8,128)(2,1)S(1)} collective-permute-done((bf16[384,512]{1,0:T(8,128)(2,1)S(1)}, bf16[384,512]{1,0:T(8,128)(2,1)S(1)}, u32[]{:S(2)}, u32[]{:S(2)}) %collective-permute-start.2) | collective-permute-done | bytes 393248 | tf_op jit(solution)/shard_map/ppermute | solution.py:319
  115.7 3.4 %answer.1 = (bf16[1024,512]{1,0:T(8,128)(2,1)}, bf16[1024,512]{1,0:T(8,128)(2,1)}) custom-call(s32[1]{0:T(128)} %bitcast.14.me_ref, s32[8,256]{1,0:T(8,128)} %reshape.116.ids_ref, bf16[384,512]{1,0:T(8,128)(2,1)} %copy-done.6, bf16[384,512]{1,0:T(8,128)(2,1)} %copy-done.22, bf16[384,512]{1,0:T(8,128)(2,1)} %copy-done.23), custom_call_target="tpu_custom_call" | custom-call | flops 1073741824 | bytes 4194304 | tf_op jit(solution)/shard_map/answer/pallas_call | solution.py:231
  125.3 2.5 collective-permute-start.6
  131.4 5.9 %collective-permute-done.5.refs_2_ = bf16[512,512]{1,0:T(8,128)(2,1)} collective-permute-done((bf16[512,512]{1,0:T(8,128)(2,1)S(1)}, bf16[512,512]{1,0:T(8,128)(2,1)}, u32[]{:S(2)}, u32[]{:S(2)}) %collective-permute-start.5) | collective-permute-done | bytes 524320 | tf_op jit(solution)/shard_map/ppermute | solution.py:323
  137.3 13.4 %collective-permute-done.6.refs_3_ = bf16[512,512]{1,0:T(8,128)(2,1)} collective-permute-done((bf16[512,512]{1,0:T(8,128)(2,1)S(1)}, bf16[512,512]{1,0:T(8,128)(2,1)}, u32[]{:S(2)}, u32[]{:S(2)}) %collective-permute-start.6) | collective-permute-done | bytes 524320 | tf_op jit(solution)/shard_map/ppermute | solution.py:323
  150.7 2.3 collective-permute-done.7.refs_4_
  153.1 16.6 %edge.1 = (s16[1024,512]{1,0:T(8,128)(2,1)}, s16[1024,512]{1,0:T(8,128)(2,1)}, s16[1536,512]{1,0:T(8,128)(2,1)}) custom-call(s32[512,1]{1,0:T(8,128)} %get-tuple-element.57.slot_col, s32[1,512]{1,0:T(1,128)} %add.118.slot_row, s32[512,1]{1,0:T(8,128)} %copy.63.tail_col, s32[1,512]{1,0:T(1,128)} %bitcast.51, f32[512,512]{1,0:T(8,128)} %select_maximum_fusion.rel_ref, ...), custom_call_target="tpu_custom_call" | custom-call | flops 9663676416 | bytes 16777216 | tf_op jit(solution)/shard_map/edge/pallas_call | solution.py:186
  169.7 6.0 %all-to-all-start.3 = ((s16[64,24,512]{2,1,0:T(8,128)(2,1)}), s16[64,24,512]{2,1,0:T(8,128)(2,1)S(1)}, u32[]{:S(2)}, u32[]{:S(2)}) async-start(s16[64,24,512]{2,1,0:T(8,128)(2,1)} %bitcast.43), calls=%async_computation.3 | async-start | bytes 3145728 | tf_op jit(solution)/shard_map/all_to_all | solution.py:497
  176.4 2.4 collective-permute-done.14.refs_1_
  180.3 2.5 collective-permute-start.16
  184.3 17.7 %collective-permute-done.15.refs_2_ = s16[512,512]{1,0:T(8,128)(2,1)} collective-permute-done((s16[512,512]{1,0:T(8,128)(2,1)S(1)}, s16[512,512]{1,0:T(8,128)(2,1)}, u32[]{:S(2)}, u32[]{:S(2)}) %collective-permute-start.15) | collective-permute-done | bytes 524320 | tf_op jit(solution)/shard_map/ppermute | solution.py:323
  202.0 18.0 %collective-permute-done.16.refs_3_ = s16[512,512]{1,0:T(8,128)(2,1)} collective-permute-done((s16[512,512]{1,0:T(8,128)(2,1)S(1)}, s16[512,512]{1,0:T(8,128)(2,1)}, u32[]{:S(2)}, u32[]{:S(2)}) %collective-permute-start.16) | collective-permute-done | bytes 524320 | tf_op jit(solution)/shard_map/ppermute | solution.py:323
  221.1 7.1 %shard_map.131 = (f32[400,256]{1,0:T(8,128)}, s16[416,256]{1,0:T(8,128)(2,1)}, s16[416,256]{1,0:T(8,128)(2,1)}, s16[416,256]{1,0:T(8,128)(2,1)}) custom-call(s32[1]{0:T(128)} %bitcast.me_ref, s32[8,256]{1,0:T(8,128)} %reshape.116.ids_ref, s16[1024,512]{1,0:T(8,128)(2,1)} %get-tuple-element.31.refs_0_, s16[1024,512]{1,0:T(8,128)(2,1)} %copy-done.5, ...), custom_call_target="tpu_custom_call" | custom-call | flops 4294967296 | bytes 8388608 | tf_op jit(solution)/shard_map/pallas_call | solution.py:303
  229.4 2.5 collective-permute-start.19
  234.2 6.9 %shard_map.129 = (f32[400,256]{1,0:T(8,128)}, s16[416,256]{1,0:T(8,128)(2,1)}, s16[416,256]{1,0:T(8,128)(2,1)}, s16[416,256]{1,0:T(8,128)(2,1)}) custom-call(s32[1]{0:T(128)} %bitcast.me_ref, s32[1,1536]{1,0:T(1,128)} %reshape.110.ids_ref, s32[1,8]{1,0:T(1,128)} %neg_ref.1, s16[64,24,512]{2,1,0:T(8,128)(2,1)} %copy-done.1), custom_call_target="tpu_custom_call" | custom-call | flops 4294967296 | bytes 8388608 | tf_op jit(solution)/shard_map/pallas_call | solution.py:303
  244.8 6.4 %all-to-all-start.4 = ((f32[8,32,512]{2,1,0:T(8,128)}), f32[8,32,512]{2,1,0:T(8,128)S(1)}, u32[]{:S(2)}, u32[]{:S(2)}) async-start(f32[8,32,512]{2,1,0:T(8,128)} %bitcast.41), calls=%async_computation.4 | async-start | bytes 1048576 | tf_op jit(solution)/shard_map/all_to_all | solution.py:525
  252.2 2.4 collective-permute-start.9
  254.7 2.5 collective-permute-done.8.refs_0_
  257.2 6.1 %collective-permute-done.9.refs_1_ = s16[416,256]{1,0:T(8,128)(2,1)S(1)} collective-permute-done((s16[416,256]{1,0:T(8,128)(2,1)S(1)}, s16[416,256]{1,0:T(8,128)(2,1)S(1)}, u32[]{:S(2)}, u32[]{:S(2)}) %collective-permute-start.9) | collective-permute-done | bytes 213024 | tf_op jit(solution)/shard_map/ppermute | solution.py:315
  267.3 3.0 %collective-permute-start.12 = (s16[416,256]{1,0:T(8,128)(2,1)}, s16[416,256]{1,0:T(8,128)(2,1)S(1)}, u32[]{:S(2)}, u32[]{:S(2)}) collective-permute-start(s16[416,256]{1,0:T(8,128)(2,1)} %shard_map.130.refs_0_), channel_id=1, source_target_pairs={{0,128},{64,192},{128,0},{192,64},{1,129},{65,193},{129,1},{193,65... | collective-permute-start | bytes 638984 | tf_op jit(solution)/shard_map/ppermute | solution.py:315
  270.3 2.6 collective-permute-done.11.refs_1_
  273.0 6.0 %collective-permute-done.12.refs_2_ = s16[416,256]{1,0:T(8,128)(2,1)S(1)} collective-permute-done((s16[416,256]{1,0:T(8,128)(2,1)}, s16[416,256]{1,0:T(8,128)(2,1)S(1)}, u32[]{:S(2)}, u32[]{:S(2)}) %collective-permute-start.12) | collective-permute-done | bytes 213024 | tf_op jit(solution)/shard_map/ppermute | solution.py:315
  279.9 3.4 %update.1 = (f32[400,1024]{1,0:T(8,128)}, f32[1,1024]{1,0:T(1,128)}) custom-call(s32[1]{0:T(128)} %bitcast.me_ref, f32[400,1024]{1,0:T(8,128)} %bitcast.40, f32[1,1024]{1,0:T(1,128)} %bitcast.52, s16[416,256]{1,0:T(8,128)(2,1)} %shard_map.130.refs_0_, s16[416,256]{1,0:T(8,128)(2,1)} %copy-done.13, s16[416,256]{1,0:T(8,128)(2,1)} %copy-done.14, ...), custom_call_target="tpu_custom_call" | custom-call | tf_op jit(solution)/shard_map/update/pallas_call | solution.py:374
  283.9 4.1 %collective-permute-start.22 = (f32[32,512]{1,0:T(8,128)S(1)}, f32[32,512]{1,0:T(8,128)S(1)}, u32[]{:S(2)}, u32[]{:S(2)}) collective-permute-start(f32[32,512]{1,0:T(8,128)S(1)} %reduce_sum.48), channel_id=1, source_target_pairs={{0,128},{64,192},{128,0},{192,64},{1,129},{65,193},{129,1},{193,65... | collective-permute-start | bytes 196616 | tf_op jit(solution)/shard_map/ppermute | solution.py:315
  (159 shorter events, 48.4 us)
Async XLA Ops:
  0.6 22.7 %copy-start = (f32[1024,400]{0,1:T(8,128)S(1)}, f32[1024,400]{0,1:T(8,128)}, u32[]{:S(2)}) copy-start(f32[1024,400]{0,1:T(8,128)} %param.10) | copy-start | bytes 4915204
  2.7 30.7 %collective-permute-start.1 = (bf16[128,512]{1,0:T(8,128)(2,1)S(1)}, bf16[128,512]{1,0:T(8,128)(2,1)S(1)}, u32[]{:S(2)}, u32[]{:S(2)}) collective-permute-start(bf16[128,512]{1,0:T(8,128)(2,1)S(1)} %pad_maximum_fusion.5), channel_id=1, source_target_pairs={{0,56},{1,57},{2,58},{3,59},{4,60},{5,61},{6,62},{7,63},{8,0},{9,1... | collective-permute-start | bytes 393224 | tf_op jit(solution)/shard_map/ppermute | solution.py:319
  9.1 24.2 %collective-permute-start = (bf16[128,512]{1,0:T(8,128)(2,1)S(1)}, bf16[128,512]{1,0:T(8,128)(2,1)}, u32[]{:S(2)}, u32[]{:S(2)}) collective-permute-start(bf16[128,512]{1,0:T(8,128)(2,1)S(1)} %pad_maximum_fusion.5), channel_id=1, source_target_pairs={{0,8},{1,9},{2,10},{3,11},{4,12},{5,13},{6,14},{7,15},{8,16},{9,17... | collective-permute-start | bytes 393224 | tf_op jit(solution)/shard_map/ppermute | solution.py:319
  14.5 18.1 %all-to-all-start = ((s32[64,1,16]{2,1,0:T(1,128)}), s32[64,1,16]{2,1,0:T(1,128)S(1)}, u32[]{:S(2)}, u32[]{:S(2)}) async-start(s32[64,1,16]{2,1,0:T(1,128)} %bitcast.6), calls=%async_computation | async-start | bytes 65536 | tf_op jit(solution)/shard_map/all_to_all | solution.py:479
  34.3 20.0 %copy-start.6 = (bf16[384,512]{1,0:T(8,128)(2,1)}, bf16[384,512]{1,0:T(8,128)(2,1)S(1)}, u32[]{:S(2)}) copy-start(bf16[384,512]{1,0:T(8,128)(2,1)S(1)} %pad_maximum_fusion.3.here) | copy-start | bytes 1179652
  36.7 8.6 %all-to-all-start.2 = ((s32[8,1,256]{2,1,0:T(1,128)}), s32[8,1,256]{2,1,0:T(1,128)S(1)}, u32[]{:S(2)}, u32[]{:S(2)}) async-start(s32[8,1,256]{2,1,0:T(1,128)} %all_to_all.31), calls=%async_computation.2 | async-start | bytes 16384 | tf_op jit(solution)/shard_map/all_to_all | solution.py:480
  45.2 107.8 %all-to-all-start.1 = ((bf16[64,24,512]{2,1,0:T(8,128)(2,1)}), bf16[64,24,512]{2,1,0:T(8,128)(2,1)}, u32[]{:S(2)}, u32[]{:S(2)}) async-start(bf16[64,24,512]{2,1,0:T(8,128)(2,1)} %bitcast.42), calls=%async_computation.1 | async-start | bytes 3145728 | tf_op jit(solution)/shard_map/all_to_all | solution.py:489
  51.0 63.8 %collective-permute-start.2 = (bf16[384,512]{1,0:T(8,128)(2,1)S(1)}, bf16[384,512]{1,0:T(8,128)(2,1)S(1)}, u32[]{:S(2)}, u32[]{:S(2)}) collective-permute-start(bf16[384,512]{1,0:T(8,128)(2,1)S(1)} %pad_maximum_fusion.3.here), channel_id=1, source_target_pairs={{0,24},{1,25},{2,26},{3,27},{4,28},{5,29},{6,30},{7,31},{8,32},{9,... | collective-permute-start | bytes 1179656 | tf_op jit(solution)/shard_map/ppermute | solution.py:319
  54.3 60.5 %collective-permute-start.3 = (bf16[384,512]{1,0:T(8,128)(2,1)S(1)}, bf16[384,512]{1,0:T(8,128)(2,1)S(1)}, u32[]{:S(2)}, u32[]{:S(2)}) collective-permute-start(bf16[384,512]{1,0:T(8,128)(2,1)S(1)} %pad_maximum_fusion.3.here), channel_id=1, source_target_pairs={{0,40},{1,41},{2,42},{3,43},{4,44},{5,45},{6,46},{7,47},{8,48},{9,... | collective-permute-start | bytes 1179656 | tf_op jit(solution)/shard_map/ppermute | solution.py:319
  119.0 3.6 %collective-permute-start.4 = (bf16[1024,512]{1,0:T(8,128)(2,1)}, bf16[1024,512]{1,0:T(8,128)(2,1)}, u32[]{:S(2)}, u32[]{:S(2)}) collective-permute-start(bf16[1024,512]{1,0:T(8,128)(2,1)} %get-tuple-element.23), channel_id=1, source_target_pairs={{0,1},{1,0},{2,3},{3,2},{4,5},{5,4},{6,7},{7,6},{8,9},{9,8},{10,11... | collective-permute-start | bytes 3145736 | tf_op jit(solution)/shard_map/ppermute | solution.py:323
  123.8 13.5 %collective-permute-start.5 = (bf16[512,512]{1,0:T(8,128)(2,1)S(1)}, bf16[512,512]{1,0:T(8,128)(2,1)}, u32[]{:S(2)}, u32[]{:S(2)}) collective-permute-start(bf16[512,512]{1,0:T(8,128)(2,1)S(1)} %pad_maximum_fusion), channel_id=1, source_target_pairs={{0,2},{1,3},{2,0},{3,1},{4,6},{5,7},{6,4},{7,5},{8,10},{9,11},{10,... | collective-permute-start | bytes 1572872 | tf_op jit(solution)/shard_map/ppermute | solution.py:323
  125.3 25.4 %collective-permute-start.6 = (bf16[512,512]{1,0:T(8,128)(2,1)S(1)}, bf16[512,512]{1,0:T(8,128)(2,1)}, u32[]{:S(2)}, u32[]{:S(2)}) collective-permute-start(bf16[512,512]{1,0:T(8,128)(2,1)S(1)} %pad_maximum_fusion.1), channel_id=1, source_target_pairs={{0,4},{1,5},{2,6},{3,7},{4,0},{5,1},{6,2},{7,3},{8,12},{9,13},{10,... | collective-permute-start | bytes 1572872 | tf_op jit(solution)/shard_map/ppermute | solution.py:323
  127.9 25.2 %collective-permute-start.7 = (bf16[512,512]{1,0:T(8,128)(2,1)S(1)}, bf16[512,512]{1,0:T(8,128)(2,1)}, u32[]{:S(2)}, u32[]{:S(2)}) collective-permute-start(bf16[512,512]{1,0:T(8,128)(2,1)S(1)} %pad_maximum_fusion.2), channel_id=1, source_target_pairs={{0,6},{1,7},{2,4},{3,5},{4,2},{5,3},{6,0},{7,1},{8,14},{9,15},{10,... | collective-permute-start | bytes 1572872 | tf_op jit(solution)/shard_map/ppermute | solution.py:323
  130.6 22.5 %copy-start.16 = (s32[512]{0:T(512)}, s32[512]{0:T(512)S(1)}, u32[]{:S(2)}) copy-start(s32[512]{0:T(512)S(1)} %fusion.22) | copy-start | bytes 6148
  169.7 63.4 %all-to-all-start.3 = ((s16[64,24,512]{2,1,0:T(8,128)(2,1)}), s16[64,24,512]{2,1,0:T(8,128)(2,1)S(1)}, u32[]{:S(2)}, u32[]{:S(2)}) async-start(s16[64,24,512]{2,1,0:T(8,128)(2,1)} %bitcast.43), calls=%async_computation.3 | async-start | bytes 3145728 | tf_op jit(solution)/shard_map/all_to_all | solution.py:497
  175.7 3.2 %collective-permute-start.14 = (s16[1024,512]{1,0:T(8,128)(2,1)}, s16[1024,512]{1,0:T(8,128)(2,1)S(1)}, u32[]{:S(2)}, u32[]{:S(2)}) collective-permute-start(s16[1024,512]{1,0:T(8,128)(2,1)} %get-tuple-element.32), channel_id=1, source_target_pairs={{0,1},{1,0},{2,3},{3,2},{4,5},{5,4},{6,7},{7,6},{8,9},{9,8},{10,11... | collective-permute-start | bytes 3145736 | tf_op jit(solution)/shard_map/ppermute | solution.py:323
  179.0 23.0 %collective-permute-start.15 = (s16[512,512]{1,0:T(8,128)(2,1)S(1)}, s16[512,512]{1,0:T(8,128)(2,1)}, u32[]{:S(2)}, u32[]{:S(2)}) collective-permute-start(s16[512,512]{1,0:T(8,128)(2,1)S(1)} %pad_add_fusion), channel_id=1, source_target_pairs={{0,2},{1,3},{2,0},{3,1},{4,6},{5,7},{6,4},{7,5},{8,10},{9,11},{10,... | collective-permute-start | bytes 1572872 | tf_op jit(solution)/shard_map/ppermute | solution.py:323
  180.3 39.7 %collective-permute-start.16 = (s16[512,512]{1,0:T(8,128)(2,1)S(1)}, s16[512,512]{1,0:T(8,128)(2,1)}, u32[]{:S(2)}, u32[]{:S(2)}) collective-permute-start(s16[512,512]{1,0:T(8,128)(2,1)S(1)} %pad_add_fusion.1), channel_id=1, source_target_pairs={{0,4},{1,5},{2,6},{3,7},{4,0},{5,1},{6,2},{7,3},{8,12},{9,13},{10,... | collective-permute-start | bytes 1572872 | tf_op jit(solution)/shard_map/ppermute | solution.py:323
  182.8 38.3 %collective-permute-start.17 = (s16[512,512]{1,0:T(8,128)(2,1)S(1)}, s16[512,512]{1,0:T(8,128)(2,1)}, u32[]{:S(2)}, u32[]{:S(2)}) collective-permute-start(s16[512,512]{1,0:T(8,128)(2,1)S(1)} %pad_add_fusion.2), channel_id=1, source_target_pairs={{0,6},{1,7},{2,4},{3,5},{4,2},{5,3},{6,0},{7,1},{8,14},{9,15},{10,... | collective-permute-start | bytes 1572872 | tf_op jit(solution)/shard_map/ppermute | solution.py:323
  228.2 12.9 %collective-permute-start.18 = (s16[416,256]{1,0:T(8,128)(2,1)}, s16[416,256]{1,0:T(8,128)(2,1)S(1)}, u32[]{:S(2)}, u32[]{:S(2)}) collective-permute-start(s16[416,256]{1,0:T(8,128)(2,1)} %get-tuple-element.35), channel_id=1, source_target_pairs={{0,64},{64,128},{128,192},{192,0},{1,65},{65,129},{129,193},{193,1... | collective-permute-start | bytes 638984 | tf_op jit(solution)/shard_map/ppermute | solution.py:315
  229.4 11.7 %collective-permute-start.19 = (s16[416,256]{1,0:T(8,128)(2,1)}, s16[416,256]{1,0:T(8,128)(2,1)S(1)}, u32[]{:S(2)}, u32[]{:S(2)}) collective-permute-start(s16[416,256]{1,0:T(8,128)(2,1)} %get-tuple-element.36), channel_id=1, source_target_pairs={{0,128},{64,192},{128,0},{192,64},{1,129},{65,193},{129,1},{193,65... | collective-permute-start | bytes 638984 | tf_op jit(solution)/shard_map/ppermute | solution.py:315
  231.9 9.2 %collective-permute-start.20 = (s16[416,256]{1,0:T(8,128)(2,1)}, s16[416,256]{1,0:T(8,128)(2,1)S(1)}, u32[]{:S(2)}, u32[]{:S(2)}) collective-permute-start(s16[416,256]{1,0:T(8,128)(2,1)} %get-tuple-element.37), channel_id=1, source_target_pairs={{0,192},{64,0},{128,64},{192,128},{1,193},{65,1},{129,65},{193,129... | collective-permute-start | bytes 638984 | tf_op jit(solution)/shard_map/ppermute | solution.py:315
  244.8 38.6 %all-to-all-start.4 = ((f32[8,32,512]{2,1,0:T(8,128)}), f32[8,32,512]{2,1,0:T(8,128)S(1)}, u32[]{:S(2)}, u32[]{:S(2)}) async-start(f32[8,32,512]{2,1,0:T(8,128)} %bitcast.41), calls=%async_computation.4 | async-start | bytes 1048576 | tf_op jit(solution)/shard_map/all_to_all | solution.py:525
  251.2 6.0 %collective-permute-start.8 = (s16[416,256]{1,0:T(8,128)(2,1)S(1)}, s16[416,256]{1,0:T(8,128)(2,1)S(1)}, u32[]{:S(2)}, u32[]{:S(2)}) collective-permute-start(s16[416,256]{1,0:T(8,128)(2,1)S(1)} %copy-done.26), channel_id=1, source_target_pairs={{0,64},{64,128},{128,192},{192,0},{1,65},{65,129},{129,193},{193,1... | collective-permute-start | bytes 638984 | tf_op jit(solution)/shard_map/ppermute | solution.py:315
  252.2 11.1 %collective-permute-start.9 = (s16[416,256]{1,0:T(8,128)(2,1)S(1)}, s16[416,256]{1,0:T(8,128)(2,1)S(1)}, u32[]{:S(2)}, u32[]{:S(2)}) collective-permute-start(s16[416,256]{1,0:T(8,128)(2,1)S(1)} %copy-done.25), channel_id=1, source_target_pairs={{0,128},{64,192},{128,0},{192,64},{1,129},{65,193},{129,1},{193,65... | collective-permute-start | bytes 638984 | tf_op jit(solution)/shard_map/ppermute | solution.py:315
  254.6 8.7 %collective-permute-start.10 = (s16[416,256]{1,0:T(8,128)(2,1)S(1)}, s16[416,256]{1,0:T(8,128)(2,1)S(1)}, u32[]{:S(2)}, u32[]{:S(2)}) collective-permute-start(s16[416,256]{1,0:T(8,128)(2,1)S(1)} %copy-done.24), channel_id=1, source_target_pairs={{0,192},{64,0},{128,64},{192,128},{1,193},{65,1},{129,65},{193,129... | collective-permute-start | bytes 638984 | tf_op jit(solution)/shard_map/ppermute | solution.py:315
  266.8 6.1 %collective-permute-start.11 = (s16[416,256]{1,0:T(8,128)(2,1)}, s16[416,256]{1,0:T(8,128)(2,1)S(1)}, u32[]{:S(2)}, u32[]{:S(2)}) collective-permute-start(s16[416,256]{1,0:T(8,128)(2,1)} %shard_map.130.refs_0_), channel_id=1, source_target_pairs={{0,64},{64,128},{128,192},{192,0},{1,65},{65,129},{129,193},{193,1... | collective-permute-start | bytes 638984 | tf_op jit(solution)/shard_map/ppermute | solution.py:315
  267.3 11.7 %collective-permute-start.12 = (s16[416,256]{1,0:T(8,128)(2,1)}, s16[416,256]{1,0:T(8,128)(2,1)S(1)}, u32[]{:S(2)}, u32[]{:S(2)}) collective-permute-start(s16[416,256]{1,0:T(8,128)(2,1)} %shard_map.130.refs_0_), channel_id=1, source_target_pairs={{0,128},{64,192},{128,0},{192,64},{1,129},{65,193},{129,1},{193,65... | collective-permute-start | bytes 638984 | tf_op jit(solution)/shard_map/ppermute | solution.py:315
  270.3 8.9 %collective-permute-start.13 = (s16[416,256]{1,0:T(8,128)(2,1)}, s16[416,256]{1,0:T(8,128)(2,1)S(1)}, u32[]{:S(2)}, u32[]{:S(2)}) collective-permute-start(s16[416,256]{1,0:T(8,128)(2,1)} %shard_map.130.refs_0_), channel_id=1, source_target_pairs={{0,192},{64,0},{128,64},{192,128},{1,193},{65,1},{129,65},{193,129... | collective-permute-start | bytes 638984 | tf_op jit(solution)/shard_map/ppermute | solution.py:315
  283.4 5.0 %collective-permute-start.21 = (f32[32,512]{1,0:T(8,128)S(1)}, f32[32,512]{1,0:T(8,128)S(1)}, u32[]{:S(2)}, u32[]{:S(2)}) collective-permute-start(f32[32,512]{1,0:T(8,128)S(1)} %reduce_sum.48), channel_id=1, source_target_pairs={{0,64},{64,128},{128,192},{192,0},{1,65},{65,129},{129,193},{193,1... | collective-permute-start | bytes 196616 | tf_op jit(solution)/shard_map/ppermute | solution.py:315
  283.9 6.5 %collective-permute-start.22 = (f32[32,512]{1,0:T(8,128)S(1)}, f32[32,512]{1,0:T(8,128)S(1)}, u32[]{:S(2)}, u32[]{:S(2)}) collective-permute-start(f32[32,512]{1,0:T(8,128)S(1)} %reduce_sum.48), channel_id=1, source_target_pairs={{0,128},{64,192},{128,0},{192,64},{1,129},{65,193},{129,1},{193,65... | collective-permute-start | bytes 196616 | tf_op jit(solution)/shard_map/ppermute | solution.py:315
  288.0 3.9 %collective-permute-start.23 = (f32[32,512]{1,0:T(8,128)S(1)}, f32[32,512]{1,0:T(8,128)S(1)}, u32[]{:S(2)}, u32[]{:S(2)}) collective-permute-start(f32[32,512]{1,0:T(8,128)S(1)} %reduce_sum.48), channel_id=1, source_target_pairs={{0,192},{64,0},{128,64},{192,128},{1,193},{65,1},{129,65},{193,129... | collective-permute-start | bytes 196616 | tf_op jit(solution)/shard_map/ppermute | solution.py:315
  (25 other events, 100.5 us)

commit v2 on v1

--- a/solution.py
+++ b/solution.py
@@ -109,29 +109,27 @@
 
 def edge_kernel(slot_col, slot_row, tail_col, tail_row, rel_ref, rows_ref, *refs):
     pieces, (same_msg, other_msg, back_msg) = refs[:5], refs[5:8]
-    found, negs, hi_buf, lo_buf, head_buf, neg_buf = refs[8:]
+    found, heads, negs, hi_buf, lo_buf, head_buf, neg_buf = refs[8:]
     edges = slot_col.shape[0]
-    slots = rows_ref.shape[0]
+    owners, per, _ = rows_ref.shape
+    slots = heads.shape[0]
     part = found.shape[0] // GROUP
-    per = slots // (GROUP * GROUP)
     n_neg = negs.shape[0]
     found[:part, :] = pieces[0][:part, :]
     found[part : 2 * part, :] = pieces[1][:part, :]
     for y in range(1, GROUP // 2):
         found[2 * y * part : 2 * (y + 1) * part, :] = pieces[y + 1][...]
     halves = 2
-    e_half, s_half, n_half = edges // halves, slots // halves, n_neg // halves
-    j = lax.broadcasted_iota(I32, (n_half, 1), 0)
-    neg_col = (j >> 3) * per + HEAD_CAP + (j & 7)
-    j = lax.broadcasted_iota(I32, (1, n_half), 1)
-    neg_row = (j >> 3) * per + HEAD_CAP + (j & 7)
+    e_half, o_half = edges // halves, owners // halves
+    s_half, n_half = slots // halves, n_neg // halves
 
     @pl.loop(0, halves)
     def _(c):
-        at = pl.ds(pl.multiple_of(c * s_half, s_half), s_half)
-        pick = (neg_col == lax.broadcasted_iota(I32, (n_half, s_half), 1)).astype(BF)
+        rows = rows_ref[pl.ds(pl.multiple_of(c * o_half, o_half), o_half)].astype(F32)
+        to = pl.ds(pl.multiple_of(c * s_half, s_half), s_half)
+        heads[to, :] = rows[:, :HEAD_CAP, :].reshape(s_half, FULL).astype(BF)
         to = pl.ds(pl.multiple_of(c * n_half, n_half), n_half)
-        negs[to, :] = dot(pick, rows_ref[at, :], MM).astype(BF)
+        negs[to, :] = rows[:, HEAD_CAP:, :].reshape(n_half, FULL).astype(BF)
 
     neg_buf[...] = jnp.zeros_like(neg_buf)
 
@@ -142,7 +140,7 @@
         pick = tail_col[at, :] == lax.broadcasted_iota(I32, (e_half, GROUP * part), 1)
         tail_f = dot(pick.astype(BF), found[...], MM)
         pick = slot_col[at, :] == lax.broadcasted_iota(I32, (e_half, slots), 1)
-        head_f = dot(pick.astype(BF), rows_ref[...], MM)
+        head_f = dot(pick.astype(BF), heads[...], MM)
         negatives = negs[...]
         queries = with_rel(rel, head_f)
         probes = against_rel(rel, tail_f)
@@ -171,26 +169,27 @@
 
     @pl.loop(0, halves)
     def _(c):
-        to = pl.ds(pl.multiple_of(c * s_half, s_half), s_half)
         back = dot(mask_of((s_half, edges), slot_row[...], c * s_half), head_buf[...], MM)
         grads = neg_buf[pl.ds(pl.multiple_of(c * n_half, n_half), n_half), :]
-        back = back + two_part_dot(mask_of((s_half, n_half), neg_row), grads)
-        back_msg[to, :] = packed(back)
+        back = [back.reshape(o_half, HEAD_CAP, FULL), grads.reshape(o_half, per - HEAD_CAP, FULL)]
+        to = pl.ds(pl.multiple_of(c * o_half, o_half), o_half)
+        back_msg[to] = packed(jnp.concatenate(back, axis=1))
 
 
 def edge_call(head_slot, tail_slot, rel, rows, pieces):
     edges = head_slot.shape[0]
-    slots = rows.shape[0]
+    owners, per, _ = rows.shape
     part = pieces[1].shape[0] * 2 // GROUP
-    n_neg = slots - GROUP * GROUP * HEAD_CAP
+    n_neg = owners * (per - HEAD_CAP)
     outs = pl.pallas_call(
         edge_kernel,
         in_specs=[vmem()] * (6 + len(pieces)),
         out_specs=[vmem()] * 3,
         out_shape=[jax.ShapeDtypeStruct((GROUP // 2 * part, FULL), I16)] * 2
-        + [jax.ShapeDtypeStruct((slots, FULL), I16)],
+        + [jax.ShapeDtypeStruct((owners, per, FULL), I16)],
         scratch_shapes=[
             pltpu.VMEM((GROUP * part, FULL), BF),
+            pltpu.VMEM((owners * HEAD_CAP, FULL), BF),
             pltpu.VMEM((n_neg, FULL), BF),
             pltpu.VMEM((edges, FULL), BF),
             pltpu.VMEM((edges, FULL), BF),
@@ -279,12 +278,12 @@
     back = unpacked(back_ref[...])
     negs = per - HEAD_CAP
     neg_sum = jnp.sum(back[:, HEAD_CAP:, :], axis=0)
-    flat[...] = back.reshape(n_src * per, FULL).astype(BF)
+    flat[...] = back[:, :HEAD_CAP, :].reshape(n_src * HEAD_CAP, FULL).astype(BF)
     hi = neg_sum.astype(BF)
     rest = neg_sum - hi.astype(F32)
 
     def src(q):
-        mask = mask_of((quarter, n_src * per), ids_ref[...], q * quarter)
+        mask = mask_of((quarter, n_src * HEAD_CAP), ids_ref[...], q * quarter)
         neg_mask = mask_of((quarter, negs), neg_ref[...], q * quarter)
         return dot(mask, flat[...], MM) + dot(neg_mask, hi, MM) + two_part_dot(neg_mask, rest)
 
@@ -384,27 +383,33 @@
     return new_table.T, new_state[0]
 
 
-def pick_kernel(ids_ref, table_ref, out_ref):
+def pick_kernel(ids_ref, neg_ref, table_ref, out_ref):
     rows = table_ref.shape[0]
-    slots = out_ref.shape[0]
-    step = 512
-
-    @pl.loop(0, slots // step)
+    negs = neg_ref.shape[0]
+    dests = 32
+    step = dests * HEAD_CAP
+    mask = (neg_ref[...] == lax.broadcasted_iota(I32, (negs, rows), 1)).astype(BF)
+    neg_rows = jnp.broadcast_to(dot(mask, table_ref[...], MM)[None], (dests, negs, FULL))
+
+    @pl.loop(0, out_ref.shape[0] // dests)
     def _(c):
         at = pl.ds(pl.multiple_of(c * step, step), step)
-        out_ref[at, :] = dot(mask_of((rows, step), ids_ref[:, at]), table_ref[...], TN).astype(BF)
-
-
-def pick_call(ids, table):
-    slots = ids.shape[1]
+        mask = (ids_ref[at, :] == lax.broadcasted_iota(I32, (step, rows), 1)).astype(BF)
+        found = dot(mask, table_ref[...], MM).reshape(dests, HEAD_CAP, FULL)
+        to = pl.ds(pl.multiple_of(c * dests, dests), dests)
+        out_ref[to] = jnp.concatenate([found, neg_rows], axis=1).astype(BF)
+
+
+def pick_call(ids, neg_ids, table):
+    dests = ids.shape[0] // HEAD_CAP
     return pl.pallas_call(
         pick_kernel,
-        in_specs=[vmem()] * 2,
+        in_specs=[vmem()] * 3,
         out_specs=vmem(),
-        out_shape=jax.ShapeDtypeStruct((slots, FULL), BF),
+        out_shape=jax.ShapeDtypeStruct((dests, HEAD_CAP + neg_ids.shape[0], FULL), BF),
         cost_estimate=pl.CostEstimate(flops=2 << 30, bytes_accessed=3 << 20, transcendentals=0),
         name="pick",
-    )(ids, table)
+    )(ids, neg_ids, table)
 
 
 def adagrad(weights, state, grad):
@@ -431,11 +436,9 @@
     width = cold_table.shape[1]
     cold_rows = cold_table.shape[0]
     hot_rows = hot_table.shape[0]
-    negs = neg_ids.shape[1]
     near = [[z * GROUP + g for g in range(GROUP)] for z in range(n_ring)]
     far = [[z * GROUP + g for z in range(n_ring)] for g in range(GROUP)]
 
-    per = HEAD_CAP + negs
     me = lax.axis_index("rep").astype(I32).reshape(1)
 
     place = lax.axis_index("table").astype(I32)
@@ -454,7 +457,7 @@
     col = lax.broadcasted_iota(jnp.int32, (edges, edges), 1)
     before = dot((col < row).astype(BF), owner_hot, ((1,), (0,)))
     rank = jnp.sum(before * owner_hot.astype(F32), axis=1).astype(jnp.int32)
-    head_slot = head_owner[:, 0] * per + rank
+    head_slot = head_owner[:, 0] * HEAD_CAP + rank
 
     edge_tail, _ = lax.optimization_barrier((edge_tail, here))
     block = edge_tail // hot_rows
@@ -475,26 +478,24 @@
     slot_rows = jnp.sum(jnp.where(match, row_iota, 0), axis=1) - 1
     slot_rows = slot_rows.reshape(n_ring, GROUP, TAIL_CAP).transpose(1, 0, 2)
 
-    wanted = jnp.zeros((n_table * per,), I32).at[head_slot].set(head_row).reshape(n_table, per)
-    wanted = lax.all_to_all(wanted[:, :HEAD_CAP], "table", 0, 0)
+    wanted = jnp.zeros((n_table * HEAD_CAP,), I32).at[head_slot].set(head_row)
+    wanted = wanted.reshape(n_table, HEAD_CAP)
+    wanted = lax.all_to_all(wanted, "table", 0, 0)
     dense_rows = lax.all_to_all(
         slot_rows.reshape(GROUP, n_ring * TAIL_CAP), "table", 0, 0, axis_index_groups=near
     )
     dense_ids = dense_rows.reshape(GROUP, n_ring, TAIL_CAP)[jnp.arange(GROUP) ^ near_me]
     dense_ids = dense_ids.transpose(1, 0, 2).reshape(n_ring, GROUP * TAIL_CAP)
-    own_negs = jnp.broadcast_to(neg_ids[0][None, :], (n_table, negs))
-    asked = jnp.concatenate([wanted, own_negs], axis=1)
-    head_ids = jnp.concatenate([wanted, jnp.full((n_table, negs), -1, I32)], axis=1)
-    picked = pick_call(asked.reshape(1, n_table * per), cold_bf)
-    rows = lax.all_to_all(picked.reshape(n_table, per, FULL), "table", 0, 0)
+    picked = pick_call(wanted.reshape(n_table * HEAD_CAP, 1), neg_ids.T, cold_bf)
+    rows = lax.all_to_all(picked, "table", 0, 0)
     relation = widen(relations[edge_rel])
     found = answer_call(ring_me, dense_ids, (here, behind, ahead))
     pieces = near_exchange(*found, n_table)
     same_msg, other_msg, back_msg = edge_call(
-        head_slot, tail_slot, relation, rows.reshape(n_table * per, FULL), pieces
-    )
-
-    back = lax.all_to_all(back_msg.reshape(n_table, per, FULL), "table", 0, 0)
+        head_slot, tail_slot, relation, rows, pieces
+    )
+
+    back = lax.all_to_all(back_msg, "table", 0, 0)
     tail_got = near_exchange(same_msg, other_msg, n_table)
 
     quarter = hot_rows // n_rep
@@ -511,10 +512,10 @@
     cold_own, *cold_msg = parts_call(
         cold_kernel,
         me,
-        (head_ids.reshape(1, n_table * per), neg_ids, back),
+        (wanted.reshape(1, n_table * HEAD_CAP), neg_ids, back),
         width,
         cold_rows // n_rep,
-        pltpu.VMEM((n_table * per, FULL), BF),
+        pltpu.VMEM((n_table * HEAD_CAP, FULL), BF),
         n_rep,
     )
     cold_got = []

time: 294 us -> 293 us (level)
  transfers between devices with their start and end apart: 29 -> 29, of which waited for: 18 -> 20; matrix products, arithmetic and copies ran while one was open for 6% -> 6% of each run, Pallas kernels for 9% -> 9%
where the time goes in v2:
time: 293 us; the launch traced here: 292 us
  waiting for transfers between devices  147 us (50%)
  starting transfers between devices  68.8 us (23%)
  Pallas kernels  43.7 us (15%)
  local copies, waits for them, and re-layouts  22.1 us (8%)
  other arithmetic  8.47 us (3%)
    ppermute x8, waiting for transfers between devices, near_swap(): return lax.ppermute(x, 'table', [(i, i ^ other) for i in range(n_table)])  60.3 us
    ppermute x4, waiting for transfers between devices, ring_shift(): lax.ppermute(x, 'table', [(i, (i + step * GROUP) % n_table) for i in rang...  57.7 us
    ppermute x12, waiting for transfers between devices, shift(): lax.ppermute(x, 'rep', [(i, (i + step) % n_rep) for i in range(n_rep)])  21.9 us
    ppermute x12, starting transfers between devices, shift(): lax.ppermute(x, 'rep', [(i, (i + step) % n_rep) for i in range(n_rep)])  16.3 us
    pallas_call x1, Pallas kernels, edge_call(): pl.pallas_call(edge_kernel, in_specs=[vmem()] * (6 + len(pieces)), out_sp...  14.7 us
    pallas_call x2, Pallas kernels, parts_call(): pl.pallas_call(functools.partial(kernel, n_rep=n_rep), in_specs=[smem()]...  13.4 us
    ppermute x4, starting transfers between devices, ring_shift(): lax.ppermute(x, 'table', [(i, (i + step * GROUP) % n_table) for i in rang...  11.3 us
    ppermute x8, starting transfers between devices, near_swap(): return lax.ppermute(x, 'table', [(i, i ^ other) for i in range(n_table)])  10.3 us
  transfers between devices with their start and end apart: 29, of which 20 were waited for; matrix products, arithmetic and copies ran while one was open for 6% of the time, Pallas kernels for 9%

profile of v2, /device:TPU:1, one launch (start us, length us, event | category | flops | bytes accessed | tf_op | source)
XLA Modules:
  0.0 292.1 jit_solution(13906324794137582962)
XLA Ops:
  2.7 6.5 %collective-permute-start.1 = (bf16[128,512]{1,0:T(8,128)(2,1)S(1)}, bf16[128,512]{1,0:T(8,128)(2,1)S(1)}, u32[]{:S(2)}, u32[]{:S(2)}) collective-permute-start(bf16[128,512]{1,0:T(8,128)(2,1)S(1)} %pad_maximum_fusion.5), channel_id=1, source_target_pairs={{0,56},{1,57},{2,58},{3,59},{4,60},{5,61},{6,62},{7,63},{8,0},{9,1... | collective-permute-start | bytes 393224 | tf_op jit(solution)/shard_map/ppermute | solution.py:318
  11.2 2.6 scatter_custom_fusion
  14.5 8.8 %all-to-all-start = ((s32[64,1,16]{2,1,0:T(1,128)}), s32[64,1,16]{2,1,0:T(1,128)S(1)}, u32[]{:S(2)}, u32[]{:S(2)}) async-start(s32[64,1,16]{2,1,0:T(1,128)} %bitcast.5), calls=%async_computation | async-start | bytes 65536 | tf_op jit(solution)/shard_map/all_to_all | solution.py:483
  26.0 6.6 %all-to-all-done = s32[64,1,16]{2,1,0:T(1,128)S(1)} async-done(((s32[64,1,16]{2,1,0:T(1,128)}), s32[64,1,16]{2,1,0:T(1,128)S(1)}, u32[]{:S(2)}, u32[]{:S(2)}) %all-to-all-start) | async-done | bytes 4128 | tf_op jit(solution)/shard_map/all_to_all | solution.py:483
  37.1 3.9 %all-to-all-start.2 = ((s32[8,1,256]{2,1,0:T(1,128)}), s32[8,1,256]{2,1,0:T(1,128)S(1)}, u32[]{:S(2)}, u32[]{:S(2)}) async-start(s32[8,1,256]{2,1,0:T(1,128)} %all_to_all.28), calls=%async_computation.2 | async-start | bytes 16384 | tf_op jit(solution)/shard_map/all_to_all | solution.py:484
  41.0 4.3 %pick.1 = bf16[64,24,512]{2,1,0:T(8,128)(2,1)} custom-call(s32[1024,1]{1,0:T(8,128)} %reshape.133.ids_ref, s32[8,1]{1,0:T(8,128)} %copy.66.neg_ref, bf16[1024,512]{1,0:T(8,128)(2,1)} %fusion.3.table_ref), custom_call_target="tpu_custom_call" | custom-call | flops 2147483648 | bytes 3145728 | tf_op jit(solution)/shard_map/pick/pallas_call | solution.py:405
  45.6 5.6 %all-to-all-start.1 = ((bf16[64,24,512]{2,1,0:T(8,128)(2,1)}), bf16[64,24,512]{2,1,0:T(8,128)(2,1)}, u32[]{:S(2)}, u32[]{:S(2)}) async-start(bf16[64,24,512]{2,1,0:T(8,128)(2,1)} %pick.1), calls=%async_computation.1 | async-start | bytes 3145728 | tf_op jit(solution)/shard_map/all_to_all | solution.py:490
  51.2 3.4 %collective-permute-start.2 = (bf16[384,512]{1,0:T(8,128)(2,1)S(1)}, bf16[384,512]{1,0:T(8,128)(2,1)S(1)}, u32[]{:S(2)}, u32[]{:S(2)}) collective-permute-start(bf16[384,512]{1,0:T(8,128)(2,1)S(1)} %pad_maximum_fusion.3.here), channel_id=1, source_target_pairs={{0,24},{1,25},{2,26},{3,27},{4,28},{5,29},{6,30},{7,31},{8,32},{9,... | collective-permute-start | bytes 1179656 | tf_op jit(solution)/shard_map/ppermute | solution.py:318
  57.4 57.7 %collective-permute-done.2.behind = bf16[384,512]{1,0:T(8,128)(2,1)S(1)} collective-permute-done((bf16[384,512]{1,0:T(8,128)(2,1)S(1)}, bf16[384,512]{1,0:T(8,128)(2,1)S(1)}, u32[]{:S(2)}, u32[]{:S(2)}) %collective-permute-start.2) | collective-permute-done | bytes 393248 | tf_op jit(solution)/shard_map/ppermute | solution.py:318
  116.0 3.4 %answer.1 = (bf16[1024,512]{1,0:T(8,128)(2,1)}, bf16[1024,512]{1,0:T(8,128)(2,1)}) custom-call(s32[1]{0:T(128)} %bitcast.10.me_ref, s32[8,256]{1,0:T(8,128)} %reshape.105.ids_ref, bf16[384,512]{1,0:T(8,128)(2,1)} %copy-done.6, bf16[384,512]{1,0:T(8,128)(2,1)} %copy-done.23, bf16[384,512]{1,0:T(8,128)(2,1)} %copy-done.24), custom_call_target="tpu_custom_call" | custom-call | flops 1073741824 | bytes 4194304 | tf_op jit(solution)/shard_map/answer/pallas_call | solution.py:230
  125.5 2.5 collective-permute-start.6
  131.6 5.9 %collective-permute-done.5.refs_2_ = bf16[512,512]{1,0:T(8,128)(2,1)} collective-permute-done((bf16[512,512]{1,0:T(8,128)(2,1)S(1)}, bf16[512,512]{1,0:T(8,128)(2,1)}, u32[]{:S(2)}, u32[]{:S(2)}) %collective-permute-start.5) | collective-permute-done | bytes 524320 | tf_op jit(solution)/shard_map/ppermute | solution.py:322
  137.5 13.4 %collective-permute-done.6.refs_3_ = bf16[512,512]{1,0:T(8,128)(2,1)} collective-permute-done((bf16[512,512]{1,0:T(8,128)(2,1)S(1)}, bf16[512,512]{1,0:T(8,128)(2,1)}, u32[]{:S(2)}, u32[]{:S(2)}) %collective-permute-start.6) | collective-permute-done | bytes 524320 | tf_op jit(solution)/shard_map/ppermute | solution.py:322
  151.0 2.3 collective-permute-done.7.refs_4_
  153.3 14.7 %edge.1 = (s16[1024,512]{1,0:T(8,128)(2,1)}, s16[1024,512]{1,0:T(8,128)(2,1)}, s16[64,24,512]{2,1,0:T(8,128)(2,1)}) custom-call(s32[512,1]{1,0:T(8,128)} %get-tuple-element.57.slot_col, s32[1,512]{1,0:T(1,128)} %add.116.slot_row, s32[512,1]{1,0:T(8,128)} %copy.70.tail_col, s32[1,512]{1,0:T(1,128)} %bitcast.43, f32[512,512]{1,0:T(8,128)} %select_maximum_fusion.rel_ref, ...), custom_call_target="tpu_custom_call" | custom-call | flops 9663676416 | bytes 16777216 | tf_op jit(solution)/shard_map/edge/pallas_call | solution.py:184
  167.9 6.0 %all-to-all-start.3 = ((s16[64,24,512]{2,1,0:T(8,128)(2,1)}), s16[64,24,512]{2,1,0:T(8,128)(2,1)S(1)}, u32[]{:S(2)}, u32[]{:S(2)}) async-start(s16[64,24,512]{2,1,0:T(8,128)(2,1)} %get-tuple-element.24), calls=%async_computation.3 | async-start | bytes 3145728 | tf_op jit(solution)/shard_map/all_to_all | solution.py:498
  174.7 2.4 collective-permute-done.14.refs_1_
  178.6 2.5 collective-permute-start.16
  183.8 16.5 %collective-permute-done.15.refs_2_ = s16[512,512]{1,0:T(8,128)(2,1)} collective-permute-done((s16[512,512]{1,0:T(8,128)(2,1)S(1)}, s16[512,512]{1,0:T(8,128)(2,1)}, u32[]{:S(2)}, u32[]{:S(2)}) %collective-permute-start.15) | collective-permute-done | bytes 524320 | tf_op jit(solution)/shard_map/ppermute | solution.py:322
  200.3 18.0 %collective-permute-done.16.refs_3_ = s16[512,512]{1,0:T(8,128)(2,1)} collective-permute-done((s16[512,512]{1,0:T(8,128)(2,1)S(1)}, s16[512,512]{1,0:T(8,128)(2,1)}, u32[]{:S(2)}, u32[]{:S(2)}) %collective-permute-start.16) | collective-permute-done | bytes 524320 | tf_op jit(solution)/shard_map/ppermute | solution.py:322
  219.4 7.1 %shard_map.131 = (f32[400,256]{1,0:T(8,128)}, s16[416,256]{1,0:T(8,128)(2,1)}, s16[416,256]{1,0:T(8,128)(2,1)}, s16[416,256]{1,0:T(8,128)(2,1)}) custom-call(s32[1]{0:T(128)} %bitcast.me_ref, s32[8,256]{1,0:T(8,128)} %reshape.105.ids_ref, s16[1024,512]{1,0:T(8,128)(2,1)} %get-tuple-element.31.refs_0_, s16[1024,512]{1,0:T(8,128)(2,1)} %copy-done.5, ...), custom_call_target="tpu_custom_call" | custom-call | flops 4294967296 | bytes 8388608 | tf_op jit(solution)/shard_map/pallas_call | solution.py:302
  227.7 2.5 collective-permute-start.19
  232.5 6.3 %shard_map.129 = (f32[400,256]{1,0:T(8,128)}, s16[416,256]{1,0:T(8,128)(2,1)}, s16[416,256]{1,0:T(8,128)(2,1)}, s16[416,256]{1,0:T(8,128)(2,1)}) custom-call(s32[1]{0:T(128)} %bitcast.me_ref, s32[1,1024]{1,0:T(1,128)} %reshape.101.ids_ref, s32[1,8]{1,0:T(1,128)} %neg_ref.1, s16[64,24,512]{2,1,0:T(8,128)(2,1)} %copy-done.1), custom_call_target="tpu_custom_call" | custom-call | flops 4294967296 | bytes 8388608 | tf_op jit(solution)/shard_map/pallas_call | solution.py:302
  242.7 6.7 %all-to-all-start.4 = ((f32[8,32,512]{2,1,0:T(8,128)}), f32[8,32,512]{2,1,0:T(8,128)S(1)}, u32[]{:S(2)}, u32[]{:S(2)}) async-start(f32[8,32,512]{2,1,0:T(8,128)} %bitcast.35), calls=%async_computation.4 | async-start | bytes 1048576 | tf_op jit(solution)/shard_map/all_to_all | solution.py:526
  250.5 2.4 collective-permute-start.9
  253.0 2.3 collective-permute-done.8.refs_0_
  255.4 6.3 %collective-permute-done.9.refs_1_ = s16[416,256]{1,0:T(8,128)(2,1)S(1)} collective-permute-done((s16[416,256]{1,0:T(8,128)(2,1)S(1)}, s16[416,256]{1,0:T(8,128)(2,1)S(1)}, u32[]{:S(2)}, u32[]{:S(2)}) %collective-permute-start.9) | collective-permute-done | bytes 213024 | tf_op jit(solution)/shard_map/ppermute | solution.py:314
  265.7 2.7 collective-permute-start.12
  268.4 2.9 collective-permute-done.11.refs_1_
  271.3 5.7 %collective-permute-done.12.refs_2_ = s16[416,256]{1,0:T(8,128)(2,1)S(1)} collective-permute-done((s16[416,256]{1,0:T(8,128)(2,1)}, s16[416,256]{1,0:T(8,128)(2,1)S(1)}, u32[]{:S(2)}, u32[]{:S(2)}) %collective-permute-start.12) | collective-permute-done | bytes 213024 | tf_op jit(solution)/shard_map/ppermute | solution.py:314
  278.3 3.4 %update.1 = (f32[400,1024]{1,0:T(8,128)}, f32[1,1024]{1,0:T(1,128)}) custom-call(s32[1]{0:T(128)} %bitcast.me_ref, f32[400,1024]{1,0:T(8,128)} %bitcast.34, f32[1,1024]{1,0:T(1,128)} %bitcast.44, s16[416,256]{1,0:T(8,128)(2,1)} %shard_map.130.refs_0_, s16[416,256]{1,0:T(8,128)(2,1)} %copy-done.13, s16[416,256]{1,0:T(8,128)(2,1)} %copy-done.14, ...), custom_call_target="tpu_custom_call" | custom-call | tf_op jit(solution)/shard_map/update/pallas_call | solution.py:373
  282.4 3.9 %collective-permute-start.22 = (f32[32,512]{1,0:T(8,128)S(1)}, f32[32,512]{1,0:T(8,128)S(1)}, u32[]{:S(2)}, u32[]{:S(2)}) collective-permute-start(f32[32,512]{1,0:T(8,128)S(1)} %reduce_sum.48), channel_id=1, source_target_pairs={{0,128},{64,192},{128,0},{192,64},{1,129},{65,193},{129,1},{193,65... | collective-permute-start | bytes 196616 | tf_op jit(solution)/shard_map/ppermute | solution.py:314
  (160 shorter events, 51.7 us)
Async XLA Ops:
  0.6 22.7 %copy-start = (f32[1024,400]{0,1:T(8,128)S(1)}, f32[1024,400]{0,1:T(8,128)}, u32[]{:S(2)}) copy-start(f32[1024,400]{0,1:T(8,128)} %param.10) | copy-start | bytes 4915204
  2.7 31.1 %collective-permute-start.1 = (bf16[128,512]{1,0:T(8,128)(2,1)S(1)}, bf16[128,512]{1,0:T(8,128)(2,1)S(1)}, u32[]{:S(2)}, u32[]{:S(2)}) collective-permute-start(bf16[128,512]{1,0:T(8,128)(2,1)S(1)} %pad_maximum_fusion.5), channel_id=1, source_target_pairs={{0,56},{1,57},{2,58},{3,59},{4,60},{5,61},{6,62},{7,63},{8,0},{9,1... | collective-permute-start | bytes 393224 | tf_op jit(solution)/shard_map/ppermute | solution.py:318
  9.1 24.6 %collective-permute-start = (bf16[128,512]{1,0:T(8,128)(2,1)S(1)}, bf16[128,512]{1,0:T(8,128)(2,1)}, u32[]{:S(2)}, u32[]{:S(2)}) collective-permute-start(bf16[128,512]{1,0:T(8,128)(2,1)S(1)} %pad_maximum_fusion.5), channel_id=1, source_target_pairs={{0,8},{1,9},{2,10},{3,11},{4,12},{5,13},{6,14},{7,15},{8,16},{9,17... | collective-permute-start | bytes 393224 | tf_op jit(solution)/shard_map/ppermute | solution.py:318
  14.5 18.1 %all-to-all-start = ((s32[64,1,16]{2,1,0:T(1,128)}), s32[64,1,16]{2,1,0:T(1,128)S(1)}, u32[]{:S(2)}, u32[]{:S(2)}) async-start(s32[64,1,16]{2,1,0:T(1,128)} %bitcast.5), calls=%async_computation | async-start | bytes 65536 | tf_op jit(solution)/shard_map/all_to_all | solution.py:483
  34.7 19.9 %copy-start.6 = (bf16[384,512]{1,0:T(8,128)(2,1)}, bf16[384,512]{1,0:T(8,128)(2,1)S(1)}, u32[]{:S(2)}) copy-start(bf16[384,512]{1,0:T(8,128)(2,1)S(1)} %pad_maximum_fusion.3.here) | copy-start | bytes 1179652
  37.1 8.6 %all-to-all-start.2 = ((s32[8,1,256]{2,1,0:T(1,128)}), s32[8,1,256]{2,1,0:T(1,128)S(1)}, u32[]{:S(2)}, u32[]{:S(2)}) async-start(s32[8,1,256]{2,1,0:T(1,128)} %all_to_all.28), calls=%async_computation.2 | async-start | bytes 16384 | tf_op jit(solution)/shard_map/all_to_all | solution.py:484
  45.6 107.6 %all-to-all-start.1 = ((bf16[64,24,512]{2,1,0:T(8,128)(2,1)}), bf16[64,24,512]{2,1,0:T(8,128)(2,1)}, u32[]{:S(2)}, u32[]{:S(2)}) async-start(bf16[64,24,512]{2,1,0:T(8,128)(2,1)} %pick.1), calls=%async_computation.1 | async-start | bytes 3145728 | tf_op jit(solution)/shard_map/all_to_all | solution.py:490
  51.2 63.9 %collective-permute-start.2 = (bf16[384,512]{1,0:T(8,128)(2,1)S(1)}, bf16[384,512]{1,0:T(8,128)(2,1)S(1)}, u32[]{:S(2)}, u32[]{:S(2)}) collective-permute-start(bf16[384,512]{1,0:T(8,128)(2,1)S(1)} %pad_maximum_fusion.3.here), channel_id=1, source_target_pairs={{0,24},{1,25},{2,26},{3,27},{4,28},{5,29},{6,30},{7,31},{8,32},{9,... | collective-permute-start | bytes 1179656 | tf_op jit(solution)/shard_map/ppermute | solution.py:318
  54.6 60.5 %collective-permute-start.3 = (bf16[384,512]{1,0:T(8,128)(2,1)S(1)}, bf16[384,512]{1,0:T(8,128)(2,1)S(1)}, u32[]{:S(2)}, u32[]{:S(2)}) collective-permute-start(bf16[384,512]{1,0:T(8,128)(2,1)S(1)} %pad_maximum_fusion.3.here), channel_id=1, source_target_pairs={{0,40},{1,41},{2,42},{3,43},{4,44},{5,45},{6,46},{7,47},{8,48},{9,... | collective-permute-start | bytes 1179656 | tf_op jit(solution)/shard_map/ppermute | solution.py:318
  119.4 3.6 %collective-permute-start.4 = (bf16[1024,512]{1,0:T(8,128)(2,1)}, bf16[1024,512]{1,0:T(8,128)(2,1)}, u32[]{:S(2)}, u32[]{:S(2)}) collective-permute-start(bf16[1024,512]{1,0:T(8,128)(2,1)} %get-tuple-element.23), channel_id=1, source_target_pairs={{0,1},{1,0},{2,3},{3,2},{4,5},{5,4},{6,7},{7,6},{8,9},{9,8},{10,11... | collective-permute-start | bytes 3145736 | tf_op jit(solution)/shard_map/ppermute | solution.py:322
  124.2 13.3 %collective-permute-start.5 = (bf16[512,512]{1,0:T(8,128)(2,1)S(1)}, bf16[512,512]{1,0:T(8,128)(2,1)}, u32[]{:S(2)}, u32[]{:S(2)}) collective-permute-start(bf16[512,512]{1,0:T(8,128)(2,1)S(1)} %pad_maximum_fusion), channel_id=1, source_target_pairs={{0,2},{1,3},{2,0},{3,1},{4,6},{5,7},{6,4},{7,5},{8,10},{9,11},{10,... | collective-permute-start | bytes 1572872 | tf_op jit(solution)/shard_map/ppermute | solution.py:322
  125.5 25.4 %collective-permute-start.6 = (bf16[512,512]{1,0:T(8,128)(2,1)S(1)}, bf16[512,512]{1,0:T(8,128)(2,1)}, u32[]{:S(2)}, u32[]{:S(2)}) collective-permute-start(bf16[512,512]{1,0:T(8,128)(2,1)S(1)} %pad_maximum_fusion.1), channel_id=1, source_target_pairs={{0,4},{1,5},{2,6},{3,7},{4,0},{5,1},{6,2},{7,3},{8,12},{9,13},{10,... | collective-permute-start | bytes 1572872 | tf_op jit(solution)/shard_map/ppermute | solution.py:322
  128.1 25.2 %collective-permute-start.7 = (bf16[512,512]{1,0:T(8,128)(2,1)S(1)}, bf16[512,512]{1,0:T(8,128)(2,1)}, u32[]{:S(2)}, u32[]{:S(2)}) collective-permute-start(bf16[512,512]{1,0:T(8,128)(2,1)S(1)} %pad_maximum_fusion.2), channel_id=1, source_target_pairs={{0,6},{1,7},{2,4},{3,5},{4,2},{5,3},{6,0},{7,1},{8,14},{9,15},{10,... | collective-permute-start | bytes 1572872 | tf_op jit(solution)/shard_map/ppermute | solution.py:322
  130.8 22.5 %copy-start.16 = (s32[512]{0:T(512)}, s32[512]{0:T(512)S(1)}, u32[]{:S(2)}) copy-start(s32[512]{0:T(512)S(1)} %fusion.20) | copy-start | bytes 6148
  167.9 63.4 %all-to-all-start.3 = ((s16[64,24,512]{2,1,0:T(8,128)(2,1)}), s16[64,24,512]{2,1,0:T(8,128)(2,1)S(1)}, u32[]{:S(2)}, u32[]{:S(2)}) async-start(s16[64,24,512]{2,1,0:T(8,128)(2,1)} %get-tuple-element.24), calls=%async_computation.3 | async-start | bytes 3145728 | tf_op jit(solution)/shard_map/all_to_all | solution.py:498
  174.0 3.2 %collective-permute-start.14 = (s16[1024,512]{1,0:T(8,128)(2,1)}, s16[1024,512]{1,0:T(8,128)(2,1)S(1)}, u32[]{:S(2)}, u32[]{:S(2)}) collective-permute-start(s16[1024,512]{1,0:T(8,128)(2,1)} %get-tuple-element.32), channel_id=1, source_target_pairs={{0,1},{1,0},{2,3},{3,2},{4,5},{5,4},{6,7},{7,6},{8,9},{9,8},{10,11... | collective-permute-start | bytes 3145736 | tf_op jit(solution)/shard_map/ppermute | solution.py:322
  177.2 23.0 %collective-permute-start.15 = (s16[512,512]{1,0:T(8,128)(2,1)S(1)}, s16[512,512]{1,0:T(8,128)(2,1)}, u32[]{:S(2)}, u32[]{:S(2)}) collective-permute-start(s16[512,512]{1,0:T(8,128)(2,1)S(1)} %pad_add_fusion), channel_id=1, source_target_pairs={{0,2},{1,3},{2,0},{3,1},{4,6},{5,7},{6,4},{7,5},{8,10},{9,11},{10,... | collective-permute-start | bytes 1572872 | tf_op jit(solution)/shard_map/ppermute | solution.py:322
  178.6 39.7 %collective-permute-start.16 = (s16[512,512]{1,0:T(8,128)(2,1)S(1)}, s16[512,512]{1,0:T(8,128)(2,1)}, u32[]{:S(2)}, u32[]{:S(2)}) collective-permute-start(s16[512,512]{1,0:T(8,128)(2,1)S(1)} %pad_add_fusion.1), channel_id=1, source_target_pairs={{0,4},{1,5},{2,6},{3,7},{4,0},{5,1},{6,2},{7,3},{8,12},{9,13},{10,... | collective-permute-start | bytes 1572872 | tf_op jit(solution)/shard_map/ppermute | solution.py:322
  181.1 38.3 %collective-permute-start.17 = (s16[512,512]{1,0:T(8,128)(2,1)S(1)}, s16[512,512]{1,0:T(8,128)(2,1)}, u32[]{:S(2)}, u32[]{:S(2)}) collective-permute-start(s16[512,512]{1,0:T(8,128)(2,1)S(1)} %pad_add_fusion.2), channel_id=1, source_target_pairs={{0,6},{1,7},{2,4},{3,5},{4,2},{5,3},{6,0},{7,1},{8,14},{9,15},{10,... | collective-permute-start | bytes 1572872 | tf_op jit(solution)/shard_map/ppermute | solution.py:322
  226.5 12.3 %collective-permute-start.18 = (s16[416,256]{1,0:T(8,128)(2,1)}, s16[416,256]{1,0:T(8,128)(2,1)S(1)}, u32[]{:S(2)}, u32[]{:S(2)}) collective-permute-start(s16[416,256]{1,0:T(8,128)(2,1)} %get-tuple-element.35), channel_id=1, source_target_pairs={{0,64},{64,128},{128,192},{192,0},{1,65},{65,129},{129,193},{193,1... | collective-permute-start | bytes 638984 | tf_op jit(solution)/shard_map/ppermute | solution.py:314
  227.7 11.3 %collective-permute-start.19 = (s16[416,256]{1,0:T(8,128)(2,1)}, s16[416,256]{1,0:T(8,128)(2,1)S(1)}, u32[]{:S(2)}, u32[]{:S(2)}) collective-permute-start(s16[416,256]{1,0:T(8,128)(2,1)} %get-tuple-element.36), channel_id=1, source_target_pairs={{0,128},{64,192},{128,0},{192,64},{1,129},{65,193},{129,1},{193,65... | collective-permute-start | bytes 638984 | tf_op jit(solution)/shard_map/ppermute | solution.py:314
  230.2 8.9 %collective-permute-start.20 = (s16[416,256]{1,0:T(8,128)(2,1)}, s16[416,256]{1,0:T(8,128)(2,1)S(1)}, u32[]{:S(2)}, u32[]{:S(2)}) collective-permute-start(s16[416,256]{1,0:T(8,128)(2,1)} %get-tuple-element.37), channel_id=1, source_target_pairs={{0,192},{64,0},{128,64},{192,128},{1,193},{65,1},{129,65},{193,129... | collective-permute-start | bytes 638984 | tf_op jit(solution)/shard_map/ppermute | solution.py:314
  242.7 39.0 %all-to-all-start.4 = ((f32[8,32,512]{2,1,0:T(8,128)}), f32[8,32,512]{2,1,0:T(8,128)S(1)}, u32[]{:S(2)}, u32[]{:S(2)}) async-start(f32[8,32,512]{2,1,0:T(8,128)} %bitcast.35), calls=%async_computation.4 | async-start | bytes 1048576 | tf_op jit(solution)/shard_map/all_to_all | solution.py:526
  249.4 6.0 %collective-permute-start.8 = (s16[416,256]{1,0:T(8,128)(2,1)S(1)}, s16[416,256]{1,0:T(8,128)(2,1)S(1)}, u32[]{:S(2)}, u32[]{:S(2)}) collective-permute-start(s16[416,256]{1,0:T(8,128)(2,1)S(1)} %copy-done.27), channel_id=1, source_target_pairs={{0,64},{64,128},{128,192},{192,0},{1,65},{65,129},{129,193},{193,1... | collective-permute-start | bytes 638984 | tf_op jit(solution)/shard_map/ppermute | solution.py:314
  250.5 11.1 %collective-permute-start.9 = (s16[416,256]{1,0:T(8,128)(2,1)S(1)}, s16[416,256]{1,0:T(8,128)(2,1)S(1)}, u32[]{:S(2)}, u32[]{:S(2)}) collective-permute-start(s16[416,256]{1,0:T(8,128)(2,1)S(1)} %copy-done.26), channel_id=1, source_target_pairs={{0,128},{64,192},{128,0},{192,64},{1,129},{65,193},{129,1},{193,65... | collective-permute-start | bytes 638984 | tf_op jit(solution)/shard_map/ppermute | solution.py:314
  252.9 8.7 %collective-permute-start.10 = (s16[416,256]{1,0:T(8,128)(2,1)S(1)}, s16[416,256]{1,0:T(8,128)(2,1)S(1)}, u32[]{:S(2)}, u32[]{:S(2)}) collective-permute-start(s16[416,256]{1,0:T(8,128)(2,1)S(1)} %copy-done.25), channel_id=1, source_target_pairs={{0,192},{64,0},{128,64},{192,128},{1,193},{65,1},{129,65},{193,129... | collective-permute-start | bytes 638984 | tf_op jit(solution)/shard_map/ppermute | solution.py:314
  265.2 6.1 %collective-permute-start.11 = (s16[416,256]{1,0:T(8,128)(2,1)}, s16[416,256]{1,0:T(8,128)(2,1)S(1)}, u32[]{:S(2)}, u32[]{:S(2)}) collective-permute-start(s16[416,256]{1,0:T(8,128)(2,1)} %shard_map.130.refs_0_), channel_id=1, source_target_pairs={{0,64},{64,128},{128,192},{192,0},{1,65},{65,129},{129,193},{193,1... | collective-permute-start | bytes 638984 | tf_op jit(solution)/shard_map/ppermute | solution.py:314
  265.7 11.3 %collective-permute-start.12 = (s16[416,256]{1,0:T(8,128)(2,1)}, s16[416,256]{1,0:T(8,128)(2,1)S(1)}, u32[]{:S(2)}, u32[]{:S(2)}) collective-permute-start(s16[416,256]{1,0:T(8,128)(2,1)} %shard_map.130.refs_0_), channel_id=1, source_target_pairs={{0,128},{64,192},{128,0},{192,64},{1,129},{65,193},{129,1},{193,65... | collective-permute-start | bytes 638984 | tf_op jit(solution)/shard_map/ppermute | solution.py:314
  268.4 9.2 %collective-permute-start.13 = (s16[416,256]{1,0:T(8,128)(2,1)}, s16[416,256]{1,0:T(8,128)(2,1)S(1)}, u32[]{:S(2)}, u32[]{:S(2)}) collective-permute-start(s16[416,256]{1,0:T(8,128)(2,1)} %shard_map.130.refs_0_), channel_id=1, source_target_pairs={{0,192},{64,0},{128,64},{192,128},{1,193},{65,1},{129,65},{193,129... | collective-permute-start | bytes 638984 | tf_op jit(solution)/shard_map/ppermute | solution.py:314
  281.8 5.0 %collective-permute-start.21 = (f32[32,512]{1,0:T(8,128)S(1)}, f32[32,512]{1,0:T(8,128)S(1)}, u32[]{:S(2)}, u32[]{:S(2)}) collective-permute-start(f32[32,512]{1,0:T(8,128)S(1)} %reduce_sum.48), channel_id=1, source_target_pairs={{0,64},{64,128},{128,192},{192,0},{1,65},{65,129},{129,193},{193,1... | collective-permute-start | bytes 196616 | tf_op jit(solution)/shard_map/ppermute | solution.py:314
  282.4 6.4 %collective-permute-start.22 = (f32[32,512]{1,0:T(8,128)S(1)}, f32[32,512]{1,0:T(8,128)S(1)}, u32[]{:S(2)}, u32[]{:S(2)}) collective-permute-start(f32[32,512]{1,0:T(8,128)S(1)} %reduce_sum.48), channel_id=1, source_target_pairs={{0,128},{64,192},{128,0},{192,64},{1,129},{65,193},{129,1},{193,65... | collective-permute-start | bytes 196616 | tf_op jit(solution)/shard_map/ppermute | solution.py:314
  286.3 4.0 %collective-permute-start.23 = (f32[32,512]{1,0:T(8,128)S(1)}, f32[32,512]{1,0:T(8,128)S(1)}, u32[]{:S(2)}, u32[]{:S(2)}) collective-permute-start(f32[32,512]{1,0:T(8,128)S(1)} %reduce_sum.48), channel_id=1, source_target_pairs={{0,192},{64,0},{128,64},{192,128},{1,193},{65,1},{129,65},{193,129... | collective-permute-start | bytes 196616 | tf_op jit(solution)/shard_map/ppermute | solution.py:314
  (25 other events, 102.8 us)

commit v3 on v2

--- a/solution.py
+++ b/solution.py
@@ -521,13 +521,14 @@
     cold_got = []
     for k in range(1, n_rep):
         cold_got.append(shift(cold_msg[k - 1], k, n_rep))
-    hot_own, _ = lax.optimization_barrier((hot_own, cold_own))
     hot_part = sum_call(hot_own, hot_got, (n_ring * quarter, FULL), F32)
     hot_rows_got = lax.all_to_all(
         hot_part.reshape(n_ring, quarter, FULL), "table", 0, 0, axis_index_groups=far
     )
     cold_part = sum_call(cold_own, cold_got, cold_got[0].shape, I16)
-    cold_parts = [cold_part] + [shift(cold_part, k, n_rep) for k in range(1, n_rep)]
+    cold_parts = [cold_part]
+    for k in range(1, n_rep):
+        cold_parts.append(shift(cold_part, k, n_rep))
     hot_sum = jnp.sum(hot_rows_got, axis=0)
     new_cold_table, new_cold_state = cold_update(me, cold_table, cold_state, cold_parts)
 

time: 293 us -> 330 us (1.13)
  blocking collectives: 0 us -> 17.9 us
  waiting for transfers between devices: 147 us -> 164 us
    all_to_all x1, waiting for transfers between devices: 0.01 us -> 29.1 us  [per_device(): back = lax.all_to_all(back_msg, 'table', 0, 0)]
    all_to_all x0 -> x1, blocking collectives: none -> 17.9 us  [per_device(): lax.all_to_all(hot_part.reshape(n_ring, quarter, FULL), 'table', 0, 0, ax...]
    ppermute x8, waiting for transfers between devices: 60.3 us -> 46 us  [near_swap(): return lax.ppermute(x, 'table', [(i, i ^ other) for i in range(n_table)])]
    all_to_all x1 -> x0, starting transfers between devices: 6.69 us -> none  [per_device(): lax.all_to_all(hot_part.reshape(n_ring, quarter, FULL), 'table', 0, 0, ax...]
    ppermute x12, starting transfers between devices: 16.3 us -> 19.6 us  [shift(): lax.ppermute(x, 'rep', [(i, (i + step) % n_rep) for i in range(n_rep)])]
    unnamed x61 -> x59, local copies, waits for them, and re-layouts: 9.28 us -> 9.66 us
  transfers between devices with their start and end apart: 29 -> 28, of which waited for: 20 -> 19; matrix products, arithmetic and copies ran while one was open for 6% -> 6% of each run, Pallas kernels for 9% -> 2%
where the time goes in v3:
time: 330 us; the launch traced here: 328 us
  waiting for transfers between devices  164 us (50%)
  starting transfers between devices  68.2 us (21%)
  Pallas kernels  43.6 us (13%)
  local copies, waits for them, and re-layouts  23.6 us (7%)
  blocking collectives  17.9 us (5%)
  other arithmetic  8.46 us (3%)
    ppermute x4, waiting for transfers between devices, ring_shift(): lax.ppermute(x, 'table', [(i, (i + step * GROUP) % n_table) for i in rang...  57.7 us
    ppermute x8, waiting for transfers between devices, near_swap(): return lax.ppermute(x, 'table', [(i, i ^ other) for i in range(n_table)])  46 us
    all_to_all x1, waiting for transfers between devices, per_device(): back = lax.all_to_all(back_msg, 'table', 0, 0)  29.1 us
    ppermute x12, waiting for transfers between devices, shift(): lax.ppermute(x, 'rep', [(i, (i + step) % n_rep) for i in range(n_rep)])  24.3 us
    ppermute x12, starting transfers between devices, shift(): lax.ppermute(x, 'rep', [(i, (i + step) % n_rep) for i in range(n_rep)])  19.6 us
    all_to_all x1, blocking collectives, per_device(): lax.all_to_all(hot_part.reshape(n_ring, quarter, FULL), 'table', 0, 0, ax...  17.9 us
    pallas_call x1, Pallas kernels, edge_call(): pl.pallas_call(edge_kernel, in_specs=[vmem()] * (6 + len(pieces)), out_sp...  14.7 us
    pallas_call x2, Pallas kernels, parts_call(): pl.pallas_call(functools.partial(kernel, n_rep=n_rep), in_specs=[smem()]...  13.4 us
  transfers between devices with their start and end apart: 28, of which 19 were waited for; matrix products, arithmetic and copies ran while one was open for 6% of the time, Pallas kernels for 2%

profile of v3, /device:TPU:1, one launch (start us, length us, event | category | flops | bytes accessed | tf_op | source)
XLA Modules:
  0.0 327.9 jit_solution(3335731968839357000)
XLA Ops:
  2.7 6.5 %collective-permute-start.1 = (bf16[128,512]{1,0:T(8,128)(2,1)S(1)}, bf16[128,512]{1,0:T(8,128)(2,1)S(1)}, u32[]{:S(2)}, u32[]{:S(2)}) collective-permute-start(bf16[128,512]{1,0:T(8,128)(2,1)S(1)} %pad_maximum_fusion.5), channel_id=1, source_target_pairs={{0,56},{1,57},{2,58},{3,59},{4,60},{5,61},{6,62},{7,63},{8,0},{9,1... | collective-permute-start | bytes 393224 | tf_op jit(solution)/shard_map/ppermute | solution.py:318
  11.2 2.6 scatter_custom_fusion
  14.5 8.8 %all-to-all-start = ((s32[64,1,16]{2,1,0:T(1,128)}), s32[64,1,16]{2,1,0:T(1,128)S(1)}, u32[]{:S(2)}, u32[]{:S(2)}) async-start(s32[64,1,16]{2,1,0:T(1,128)} %bitcast.5), calls=%async_computation | async-start | bytes 65536 | tf_op jit(solution)/shard_map/all_to_all | solution.py:483
  26.0 6.6 %all-to-all-done = s32[64,1,16]{2,1,0:T(1,128)S(1)} async-done(((s32[64,1,16]{2,1,0:T(1,128)}), s32[64,1,16]{2,1,0:T(1,128)S(1)}, u32[]{:S(2)}, u32[]{:S(2)}) %all-to-all-start) | async-done | bytes 4128 | tf_op jit(solution)/shard_map/all_to_all | solution.py:483
  37.1 3.9 %all-to-all-start.2 = ((s32[8,1,256]{2,1,0:T(1,128)}), s32[8,1,256]{2,1,0:T(1,128)S(1)}, u32[]{:S(2)}, u32[]{:S(2)}) async-start(s32[8,1,256]{2,1,0:T(1,128)} %all_to_all.28), calls=%async_computation.2 | async-start | bytes 16384 | tf_op jit(solution)/shard_map/all_to_all | solution.py:484
  41.0 4.3 %pick.1 = bf16[64,24,512]{2,1,0:T(8,128)(2,1)} custom-call(s32[1024,1]{1,0:T(8,128)} %reshape.133.ids_ref, s32[8,1]{1,0:T(8,128)} %copy.66.neg_ref, bf16[1024,512]{1,0:T(8,128)(2,1)} %fusion.3.table_ref), custom_call_target="tpu_custom_call" | custom-call | flops 2147483648 | bytes 3145728 | tf_op jit(solution)/shard_map/pick/pallas_call | solution.py:405
  45.6 5.6 %all-to-all-start.1 = ((bf16[64,24,512]{2,1,0:T(8,128)(2,1)}), bf16[64,24,512]{2,1,0:T(8,128)(2,1)}, u32[]{:S(2)}, u32[]{:S(2)}) async-start(bf16[64,24,512]{2,1,0:T(8,128)(2,1)} %pick.1), calls=%async_computation.1 | async-start | bytes 3145728 | tf_op jit(solution)/shard_map/all_to_all | solution.py:490
  51.2 3.4 %collective-permute-start.2 = (bf16[384,512]{1,0:T(8,128)(2,1)S(1)}, bf16[384,512]{1,0:T(8,128)(2,1)S(1)}, u32[]{:S(2)}, u32[]{:S(2)}) collective-permute-start(bf16[384,512]{1,0:T(8,128)(2,1)S(1)} %pad_maximum_fusion.3.here), channel_id=1, source_target_pairs={{0,24},{1,25},{2,26},{3,27},{4,28},{5,29},{6,30},{7,31},{8,32},{9,... | collective-permute-start | bytes 1179656 | tf_op jit(solution)/shard_map/ppermute | solution.py:318
  57.4 57.7 %collective-permute-done.2.behind = bf16[384,512]{1,0:T(8,128)(2,1)S(1)} collective-permute-done((bf16[384,512]{1,0:T(8,128)(2,1)S(1)}, bf16[384,512]{1,0:T(8,128)(2,1)S(1)}, u32[]{:S(2)}, u32[]{:S(2)}) %collective-permute-start.2) | collective-permute-done | bytes 393248 | tf_op jit(solution)/shard_map/ppermute | solution.py:318
  116.0 3.4 %answer.1 = (bf16[1024,512]{1,0:T(8,128)(2,1)}, bf16[1024,512]{1,0:T(8,128)(2,1)}) custom-call(s32[1]{0:T(128)} %bitcast.10.me_ref, s32[8,256]{1,0:T(8,128)} %reshape.105.ids_ref, bf16[384,512]{1,0:T(8,128)(2,1)} %copy-done.5, bf16[384,512]{1,0:T(8,128)(2,1)} %copy-done.25, bf16[384,512]{1,0:T(8,128)(2,1)} %copy-done.26), custom_call_target="tpu_custom_call" | custom-call | flops 1073741824 | bytes 4194304 | tf_op jit(solution)/shard_map/answer/pallas_call | solution.py:230
  125.5 2.5 collective-permute-start.6
  131.6 5.9 %collective-permute-done.5.refs_2_ = bf16[512,512]{1,0:T(8,128)(2,1)} collective-permute-done((bf16[512,512]{1,0:T(8,128)(2,1)S(1)}, bf16[512,512]{1,0:T(8,128)(2,1)}, u32[]{:S(2)}, u32[]{:S(2)}) %collective-permute-start.5) | collective-permute-done | bytes 524320 | tf_op jit(solution)/shard_map/ppermute | solution.py:322
  137.4 13.4 %collective-permute-done.6.refs_3_ = bf16[512,512]{1,0:T(8,128)(2,1)} collective-permute-done((bf16[512,512]{1,0:T(8,128)(2,1)S(1)}, bf16[512,512]{1,0:T(8,128)(2,1)}, u32[]{:S(2)}, u32[]{:S(2)}) %collective-permute-start.6) | collective-permute-done | bytes 524320 | tf_op jit(solution)/shard_map/ppermute | solution.py:322
  153.2 14.7 %edge.1 = (s16[1024,512]{1,0:T(8,128)(2,1)}, s16[1024,512]{1,0:T(8,128)(2,1)}, s16[64,24,512]{2,1,0:T(8,128)(2,1)}) custom-call(s32[512,1]{1,0:T(8,128)} %get-tuple-element.55.slot_col, s32[1,512]{1,0:T(1,128)} %add.116.slot_row, s32[512,1]{1,0:T(8,128)} %copy.70.tail_col, s32[1,512]{1,0:T(1,128)} %bitcast.43, f32[512,512]{1,0:T(8,128)} %select_maximum_fusion.rel_ref, ...), custom_call_target="tpu_custom_call" | custom-call | flops 9663676416 | bytes 16777216 | tf_op jit(solution)/shard_map/edge/pallas_call | solution.py:184
  173.9 2.5 collective-permute-start.17
  176.5 9.0 %collective-permute-done.15.refs_2_ = s16[512,512]{1,0:T(8,128)(2,1)S(1)} collective-permute-done((s16[512,512]{1,0:T(8,128)(2,1)S(1)}, s16[512,512]{1,0:T(8,128)(2,1)S(1)}, u32[]{:S(2)}, u32[]{:S(2)}) %collective-permute-start.15) | collective-permute-done | bytes 524320 | tf_op jit(solution)/shard_map/ppermute | solution.py:322
  185.5 11.2 %collective-permute-done.16.refs_3_ = s16[512,512]{1,0:T(8,128)(2,1)S(1)} collective-permute-done((s16[512,512]{1,0:T(8,128)(2,1)S(1)}, s16[512,512]{1,0:T(8,128)(2,1)S(1)}, u32[]{:S(2)}, u32[]{:S(2)}) %collective-permute-start.16) | collective-permute-done | bytes 524320 | tf_op jit(solution)/shard_map/ppermute | solution.py:322
  196.7 2.3 collective-permute-done.17.refs_4_
  199.8 7.1 %shard_map.131 = (f32[400,256]{1,0:T(8,128)}, s16[416,256]{1,0:T(8,128)(2,1)}, s16[416,256]{1,0:T(8,128)(2,1)}, s16[416,256]{1,0:T(8,128)(2,1)}) custom-call(s32[1]{0:T(128)} %bitcast.me_ref, s32[8,256]{1,0:T(8,128)} %reshape.105.ids_ref, s16[1024,512]{1,0:T(8,128)(2,1)} %get-tuple-element.30.refs_0_, s16[1024,512]{1,0:T(8,128)(2,1)} %copy-done.4, ...), custom_call_target="tpu_custom_call" | custom-call | flops 4294967296 | bytes 8388608 | tf_op jit(solution)/shard_map/pallas_call | solution.py:302
  208.1 2.5 collective-permute-start.19
  213.3 5.5 %collective-permute-done.19.refs_1_ = s16[416,256]{1,0:T(8,128)(2,1)S(1)} collective-permute-done((s16[416,256]{1,0:T(8,128)(2,1)}, s16[416,256]{1,0:T(8,128)(2,1)S(1)}, u32[]{:S(2)}, u32[]{:S(2)}) %collective-permute-start.19) | collective-permute-done | bytes 213024 | tf_op jit(solution)/shard_map/ppermute | solution.py:314
  221.9 17.9 %all_to_all.34 = f32[8,32,512]{2,1,0:T(8,128)S(1)} all-to-all(f32[8,32,512]{2,1,0:T(8,128)} %bitcast.35), channel_id=1, replica_groups={{0,8,16,24,32,40,48,56},{1,9,17,25,33,41,49,57},{2,10,18,26,34,42,50,58..., dimensions={0} | all-to-all | bytes 1048576 | tf_op jit(solution)/shard_map/all_to_all | solution.py:525
  239.8 8.7 %all-to-all-start.3 = ((s16[64,24,512]{2,1,0:T(8,128)(2,1)}), s16[64,24,512]{2,1,0:T(8,128)(2,1)S(1)}, u32[]{:S(2)}, u32[]{:S(2)}) async-start(s16[64,24,512]{2,1,0:T(8,128)(2,1)} %get-tuple-element.23), calls=%async_computation.3 | async-start | bytes 3145728 | tf_op jit(solution)/shard_map/all_to_all | solution.py:498
  250.5 2.5 collective-permute-start.21
  255.6 2.6 collective-permute-done.22
  258.5 29.1 %all-to-all-done.3.back_ref = s16[64,24,512]{2,1,0:T(8,128)(2,1)S(1)} async-done(((s16[64,24,512]{2,1,0:T(8,128)(2,1)}), s16[64,24,512]{2,1,0:T(8,128)(2,1)S(1)}, u32[]{:S(2)}, u32[]{:S(2)}) %all-to-all-start.3) | async-done | bytes 1572896 | tf_op jit(solution)/shard_map/all_to_all | solution.py:498
  288.7 6.3 %shard_map.129 = (f32[400,256]{1,0:T(8,128)}, s16[416,256]{1,0:T(8,128)(2,1)}, s16[416,256]{1,0:T(8,128)(2,1)}, s16[416,256]{1,0:T(8,128)(2,1)}) custom-call(s32[1]{0:T(128)} %bitcast.me_ref, s32[1,1024]{1,0:T(1,128)} %reshape.101.ids_ref, s32[1,8]{1,0:T(1,128)} %neg_ref.1, s16[64,24,512]{2,1,0:T(8,128)(2,1)} %copy-done.1), custom_call_target="tpu_custom_call" | custom-call | flops 4294967296 | bytes 8388608 | tf_op jit(solution)/shard_map/pallas_call | solution.py:302
  295.0 2.5 collective-permute-start.8
  302.1 5.6 %collective-permute-done.9.refs_1_ = s16[416,256]{1,0:T(8,128)(2,1)S(1)} collective-permute-done((s16[416,256]{1,0:T(8,128)(2,1)}, s16[416,256]{1,0:T(8,128)(2,1)S(1)}, u32[]{:S(2)}, u32[]{:S(2)}) %collective-permute-start.9) | collective-permute-done | bytes 213024 | tf_op jit(solution)/shard_map/ppermute | solution.py:314
  310.6 2.5 collective-permute-start.11
  317.3 6.5 %collective-permute-done.12.refs_2_ = s16[416,256]{1,0:T(8,128)(2,1)S(1)} collective-permute-done((s16[416,256]{1,0:T(8,128)(2,1)}, s16[416,256]{1,0:T(8,128)(2,1)S(1)}, u32[]{:S(2)}, u32[]{:S(2)}) %collective-permute-start.12) | collective-permute-done | bytes 213024 | tf_op jit(solution)/shard_map/ppermute | solution.py:314
  324.5 3.4 %update.1 = (f32[400,1024]{1,0:T(8,128)}, f32[1,1024]{1,0:T(1,128)}) custom-call(s32[1]{0:T(128)} %bitcast.me_ref, f32[400,1024]{1,0:T(8,128)} %bitcast.34, f32[1,1024]{1,0:T(1,128)} %bitcast.44, s16[416,256]{1,0:T(8,128)(2,1)} %shard_map.130.refs_0_, s16[416,256]{1,0:T(8,128)(2,1)} %copy-done.12, s16[416,256]{1,0:T(8,128)(2,1)} %copy-done.13, ...), custom_call_target="tpu_custom_call" | custom-call | tf_op jit(solution)/shard_map/update/pallas_call | solution.py:373
  (157 shorter events, 59.8 us)
Async XLA Ops:
  0.6 22.7 %copy-start = (f32[1024,400]{0,1:T(8,128)S(1)}, f32[1024,400]{0,1:T(8,128)}, u32[]{:S(2)}) copy-start(f32[1024,400]{0,1:T(8,128)} %param.10) | copy-start | bytes 4915204
  2.7 31.1 %collective-permute-start.1 = (bf16[128,512]{1,0:T(8,128)(2,1)S(1)}, bf16[128,512]{1,0:T(8,128)(2,1)S(1)}, u32[]{:S(2)}, u32[]{:S(2)}) collective-permute-start(bf16[128,512]{1,0:T(8,128)(2,1)S(1)} %pad_maximum_fusion.5), channel_id=1, source_target_pairs={{0,56},{1,57},{2,58},{3,59},{4,60},{5,61},{6,62},{7,63},{8,0},{9,1... | collective-permute-start | bytes 393224 | tf_op jit(solution)/shard_map/ppermute | solution.py:318
  9.1 24.6 %collective-permute-start = (bf16[128,512]{1,0:T(8,128)(2,1)S(1)}, bf16[128,512]{1,0:T(8,128)(2,1)}, u32[]{:S(2)}, u32[]{:S(2)}) collective-permute-start(bf16[128,512]{1,0:T(8,128)(2,1)S(1)} %pad_maximum_fusion.5), channel_id=1, source_target_pairs={{0,8},{1,9},{2,10},{3,11},{4,12},{5,13},{6,14},{7,15},{8,16},{9,17... | collective-permute-start | bytes 393224 | tf_op jit(solution)/shard_map/ppermute | solution.py:318
  14.5 18.1 %all-to-all-start = ((s32[64,1,16]{2,1,0:T(1,128)}), s32[64,1,16]{2,1,0:T(1,128)S(1)}, u32[]{:S(2)}, u32[]{:S(2)}) async-start(s32[64,1,16]{2,1,0:T(1,128)} %bitcast.5), calls=%async_computation | async-start | bytes 65536 | tf_op jit(solution)/shard_map/all_to_all | solution.py:483
  34.7 19.9 %copy-start.5 = (bf16[384,512]{1,0:T(8,128)(2,1)}, bf16[384,512]{1,0:T(8,128)(2,1)S(1)}, u32[]{:S(2)}) copy-start(bf16[384,512]{1,0:T(8,128)(2,1)S(1)} %pad_maximum_fusion.3.here) | copy-start | bytes 1179652
  37.1 8.6 %all-to-all-start.2 = ((s32[8,1,256]{2,1,0:T(1,128)}), s32[8,1,256]{2,1,0:T(1,128)S(1)}, u32[]{:S(2)}, u32[]{:S(2)}) async-start(s32[8,1,256]{2,1,0:T(1,128)} %all_to_all.28), calls=%async_computation.2 | async-start | bytes 16384 | tf_op jit(solution)/shard_map/all_to_all | solution.py:484
  45.6 107.6 %all-to-all-start.1 = ((bf16[64,24,512]{2,1,0:T(8,128)(2,1)}), bf16[64,24,512]{2,1,0:T(8,128)(2,1)}, u32[]{:S(2)}, u32[]{:S(2)}) async-start(bf16[64,24,512]{2,1,0:T(8,128)(2,1)} %pick.1), calls=%async_computation.1 | async-start | bytes 3145728 | tf_op jit(solution)/shard_map/all_to_all | solution.py:490
  51.2 63.9 %collective-permute-start.2 = (bf16[384,512]{1,0:T(8,128)(2,1)S(1)}, bf16[384,512]{1,0:T(8,128)(2,1)S(1)}, u32[]{:S(2)}, u32[]{:S(2)}) collective-permute-start(bf16[384,512]{1,0:T(8,128)(2,1)S(1)} %pad_maximum_fusion.3.here), channel_id=1, source_target_pairs={{0,24},{1,25},{2,26},{3,27},{4,28},{5,29},{6,30},{7,31},{8,32},{9,... | collective-permute-start | bytes 1179656 | tf_op jit(solution)/shard_map/ppermute | solution.py:318
  54.6 60.5 %collective-permute-start.3 = (bf16[384,512]{1,0:T(8,128)(2,1)S(1)}, bf16[384,512]{1,0:T(8,128)(2,1)S(1)}, u32[]{:S(2)}, u32[]{:S(2)}) collective-permute-start(bf16[384,512]{1,0:T(8,128)(2,1)S(1)} %pad_maximum_fusion.3.here), channel_id=1, source_target_pairs={{0,40},{1,41},{2,42},{3,43},{4,44},{5,45},{6,46},{7,47},{8,48},{9,... | collective-permute-start | bytes 1179656 | tf_op jit(solution)/shard_map/ppermute | solution.py:318
  119.3 3.6 %collective-permute-start.4 = (bf16[1024,512]{1,0:T(8,128)(2,1)}, bf16[1024,512]{1,0:T(8,128)(2,1)}, u32[]{:S(2)}, u32[]{:S(2)}) collective-permute-start(bf16[1024,512]{1,0:T(8,128)(2,1)} %get-tuple-element.22), channel_id=1, source_target_pairs={{0,1},{1,0},{2,3},{3,2},{4,5},{5,4},{6,7},{7,6},{8,9},{9,8},{10,11... | collective-permute-start | bytes 3145736 | tf_op jit(solution)/shard_map/ppermute | solution.py:322
  124.1 13.3 %collective-permute-start.5 = (bf16[512,512]{1,0:T(8,128)(2,1)S(1)}, bf16[512,512]{1,0:T(8,128)(2,1)}, u32[]{:S(2)}, u32[]{:S(2)}) collective-permute-start(bf16[512,512]{1,0:T(8,128)(2,1)S(1)} %pad_maximum_fusion), channel_id=1, source_target_pairs={{0,2},{1,3},{2,0},{3,1},{4,6},{5,7},{6,4},{7,5},{8,10},{9,11},{10,... | collective-permute-start | bytes 1572872 | tf_op jit(solution)/shard_map/ppermute | solution.py:322
  125.5 25.4 %collective-permute-start.6 = (bf16[512,512]{1,0:T(8,128)(2,1)S(1)}, bf16[512,512]{1,0:T(8,128)(2,1)}, u32[]{:S(2)}, u32[]{:S(2)}) collective-permute-start(bf16[512,512]{1,0:T(8,128)(2,1)S(1)} %pad_maximum_fusion.1), channel_id=1, source_target_pairs={{0,4},{1,5},{2,6},{3,7},{4,0},{5,1},{6,2},{7,3},{8,12},{9,13},{10,... | collective-permute-start | bytes 1572872 | tf_op jit(solution)/shard_map/ppermute | solution.py:322
  128.0 25.2 %collective-permute-start.7 = (bf16[512,512]{1,0:T(8,128)(2,1)S(1)}, bf16[512,512]{1,0:T(8,128)(2,1)}, u32[]{:S(2)}, u32[]{:S(2)}) collective-permute-start(bf16[512,512]{1,0:T(8,128)(2,1)S(1)} %pad_maximum_fusion.2), channel_id=1, source_target_pairs={{0,6},{1,7},{2,4},{3,5},{4,2},{5,3},{6,0},{7,1},{8,14},{9,15},{10,... | collective-permute-start | bytes 1572872 | tf_op jit(solution)/shard_map/ppermute | solution.py:322
  130.7 22.5 %copy-start.15 = (s32[512]{0:T(512)}, s32[512]{0:T(512)S(1)}, u32[]{:S(2)}) copy-start(s32[512]{0:T(512)S(1)} %fusion.20) | copy-start | bytes 6148
  167.9 4.3 %collective-permute-start.14 = (s16[1024,512]{1,0:T(8,128)(2,1)}, s16[1024,512]{1,0:T(8,128)(2,1)S(1)}, u32[]{:S(2)}, u32[]{:S(2)}) collective-permute-start(s16[1024,512]{1,0:T(8,128)(2,1)} %get-tuple-element.31), channel_id=1, source_target_pairs={{0,1},{1,0},{2,3},{3,2},{4,5},{5,4},{6,7},{7,6},{8,9},{9,8},{10,11... | collective-permute-start | bytes 3145736 | tf_op jit(solution)/shard_map/ppermute | solution.py:322
  172.3 13.2 %collective-permute-start.15 = (s16[512,512]{1,0:T(8,128)(2,1)S(1)}, s16[512,512]{1,0:T(8,128)(2,1)S(1)}, u32[]{:S(2)}, u32[]{:S(2)}) collective-permute-start(s16[512,512]{1,0:T(8,128)(2,1)S(1)} %pad_add_fusion), channel_id=1, source_target_pairs={{0,2},{1,3},{2,0},{3,1},{4,6},{5,7},{6,4},{7,5},{8,10},{9,11},{10,... | collective-permute-start | bytes 1572872 | tf_op jit(solution)/shard_map/ppermute | solution.py:322
  173.2 23.5 %collective-permute-start.16 = (s16[512,512]{1,0:T(8,128)(2,1)S(1)}, s16[512,512]{1,0:T(8,128)(2,1)S(1)}, u32[]{:S(2)}, u32[]{:S(2)}) collective-permute-start(s16[512,512]{1,0:T(8,128)(2,1)S(1)} %pad_add_fusion.1), channel_id=1, source_target_pairs={{0,4},{1,5},{2,6},{3,7},{4,0},{5,1},{6,2},{7,3},{8,12},{9,13},{10,... | collective-permute-start | bytes 1572872 | tf_op jit(solution)/shard_map/ppermute | solution.py:322
  173.9 25.1 %collective-permute-start.17 = (s16[512,512]{1,0:T(8,128)(2,1)S(1)}, s16[512,512]{1,0:T(8,128)(2,1)S(1)}, u32[]{:S(2)}, u32[]{:S(2)}) collective-permute-start(s16[512,512]{1,0:T(8,128)(2,1)S(1)} %pad_add_fusion.2), channel_id=1, source_target_pairs={{0,6},{1,7},{2,4},{3,5},{4,2},{5,3},{6,0},{7,1},{8,14},{9,15},{10,... | collective-permute-start | bytes 1572872 | tf_op jit(solution)/shard_map/ppermute | solution.py:322
  206.9 6.4 %collective-permute-start.18 = (s16[416,256]{1,0:T(8,128)(2,1)}, s16[416,256]{1,0:T(8,128)(2,1)S(1)}, u32[]{:S(2)}, u32[]{:S(2)}) collective-permute-start(s16[416,256]{1,0:T(8,128)(2,1)} %get-tuple-element.33), channel_id=1, source_target_pairs={{0,64},{64,128},{128,192},{192,0},{1,65},{65,129},{129,193},{193,1... | collective-permute-start | bytes 638984 | tf_op jit(solution)/shard_map/ppermute | solution.py:314
  208.1 10.8 %collective-permute-start.19 = (s16[416,256]{1,0:T(8,128)(2,1)}, s16[416,256]{1,0:T(8,128)(2,1)S(1)}, u32[]{:S(2)}, u32[]{:S(2)}) collective-permute-start(s16[416,256]{1,0:T(8,128)(2,1)} %get-tuple-element.34), channel_id=1, source_target_pairs={{0,128},{64,192},{128,0},{192,64},{1,129},{65,193},{129,1},{193,65... | collective-permute-start | bytes 638984 | tf_op jit(solution)/shard_map/ppermute | solution.py:314
  210.5 8.3 %collective-permute-start.20 = (s16[416,256]{1,0:T(8,128)(2,1)}, s16[416,256]{1,0:T(8,128)(2,1)S(1)}, u32[]{:S(2)}, u32[]{:S(2)}) collective-permute-start(s16[416,256]{1,0:T(8,128)(2,1)} %get-tuple-element.35), channel_id=1, source_target_pairs={{0,192},{64,0},{128,64},{192,128},{1,193},{65,1},{129,65},{193,129... | collective-permute-start | bytes 638984 | tf_op jit(solution)/shard_map/ppermute | solution.py:314
  239.8 47.8 %all-to-all-start.3 = ((s16[64,24,512]{2,1,0:T(8,128)(2,1)}), s16[64,24,512]{2,1,0:T(8,128)(2,1)S(1)}, u32[]{:S(2)}, u32[]{:S(2)}) async-start(s16[64,24,512]{2,1,0:T(8,128)(2,1)} %get-tuple-element.23), calls=%async_computation.3 | async-start | bytes 3145728 | tf_op jit(solution)/shard_map/all_to_all | solution.py:498
  250.5 5.1 %collective-permute-start.21 = (f32[32,512]{1,0:T(8,128)S(1)}, f32[32,512]{1,0:T(8,128)S(1)}, u32[]{:S(2)}, u32[]{:S(2)}) collective-permute-start(f32[32,512]{1,0:T(8,128)S(1)} %reduce_sum.48), channel_id=1, source_target_pairs={{0,64},{64,128},{128,192},{192,0},{1,65},{65,129},{129,193},{193,1... | collective-permute-start | bytes 196616 | tf_op jit(solution)/shard_map/ppermute | solution.py:314
  253.1 5.1 %collective-permute-start.22 = (f32[32,512]{1,0:T(8,128)S(1)}, f32[32,512]{1,0:T(8,128)S(1)}, u32[]{:S(2)}, u32[]{:S(2)}) collective-permute-start(f32[32,512]{1,0:T(8,128)S(1)} %reduce_sum.48), channel_id=1, source_target_pairs={{0,128},{64,192},{128,0},{192,64},{1,129},{65,193},{129,1},{193,65... | collective-permute-start | bytes 196616 | tf_op jit(solution)/shard_map/ppermute | solution.py:314
  254.6 3.6 %collective-permute-start.23 = (f32[32,512]{1,0:T(8,128)S(1)}, f32[32,512]{1,0:T(8,128)S(1)}, u32[]{:S(2)}, u32[]{:S(2)}) collective-permute-start(f32[32,512]{1,0:T(8,128)S(1)} %reduce_sum.48), channel_id=1, source_target_pairs={{0,192},{64,0},{128,64},{192,128},{1,193},{65,1},{129,65},{193,129... | collective-permute-start | bytes 196616 | tf_op jit(solution)/shard_map/ppermute | solution.py:314
  258.4 41.4 %copy-start.21 = (f32[128]{0:T(128)S(1)}, f32[128]{0:T(128)}, u32[]{:S(2)}) copy-start(f32[128]{0:T(128)} %param.13) | copy-start | bytes 1540
  295.0 7.1 %collective-permute-start.8 = (s16[416,256]{1,0:T(8,128)(2,1)}, s16[416,256]{1,0:T(8,128)(2,1)S(1)}, u32[]{:S(2)}, u32[]{:S(2)}) collective-permute-start(s16[416,256]{1,0:T(8,128)(2,1)} %get-tuple-element.25), channel_id=1, source_target_pairs={{0,64},{64,128},{128,192},{192,0},{1,65},{65,129},{129,193},{193,1... | collective-permute-start | bytes 638984 | tf_op jit(solution)/shard_map/ppermute | solution.py:314
  297.5 10.2 %collective-permute-start.9 = (s16[416,256]{1,0:T(8,128)(2,1)}, s16[416,256]{1,0:T(8,128)(2,1)S(1)}, u32[]{:S(2)}, u32[]{:S(2)}) collective-permute-start(s16[416,256]{1,0:T(8,128)(2,1)} %get-tuple-element.26), channel_id=1, source_target_pairs={{0,128},{64,192},{128,0},{192,64},{1,129},{65,193},{129,1},{193,65... | collective-permute-start | bytes 638984 | tf_op jit(solution)/shard_map/ppermute | solution.py:314
  299.0 8.6 %collective-permute-start.10 = (s16[416,256]{1,0:T(8,128)(2,1)}, s16[416,256]{1,0:T(8,128)(2,1)S(1)}, u32[]{:S(2)}, u32[]{:S(2)}) collective-permute-start(s16[416,256]{1,0:T(8,128)(2,1)} %get-tuple-element.27), channel_id=1, source_target_pairs={{0,192},{64,0},{128,64},{192,128},{1,193},{65,1},{129,65},{193,129... | collective-permute-start | bytes 638984 | tf_op jit(solution)/shard_map/ppermute | solution.py:314
  310.6 6.6 %collective-permute-start.11 = (s16[416,256]{1,0:T(8,128)(2,1)}, s16[416,256]{1,0:T(8,128)(2,1)S(1)}, u32[]{:S(2)}, u32[]{:S(2)}) collective-permute-start(s16[416,256]{1,0:T(8,128)(2,1)} %shard_map.130.refs_0_), channel_id=1, source_target_pairs={{0,64},{64,128},{128,192},{192,0},{1,65},{65,129},{129,193},{193,1... | collective-permute-start | bytes 638984 | tf_op jit(solution)/shard_map/ppermute | solution.py:314
  313.1 10.6 %collective-permute-start.12 = (s16[416,256]{1,0:T(8,128)(2,1)}, s16[416,256]{1,0:T(8,128)(2,1)S(1)}, u32[]{:S(2)}, u32[]{:S(2)}) collective-permute-start(s16[416,256]{1,0:T(8,128)(2,1)} %shard_map.130.refs_0_), channel_id=1, source_target_pairs={{0,128},{64,192},{128,0},{192,64},{1,129},{65,193},{129,1},{193,65... | collective-permute-start | bytes 638984 | tf_op jit(solution)/shard_map/ppermute | solution.py:314
  314.7 9.0 %collective-permute-start.13 = (s16[416,256]{1,0:T(8,128)(2,1)}, s16[416,256]{1,0:T(8,128)(2,1)S(1)}, u32[]{:S(2)}, u32[]{:S(2)}) collective-permute-start(s16[416,256]{1,0:T(8,128)(2,1)} %shard_map.130.refs_0_), channel_id=1, source_target_pairs={{0,192},{64,0},{128,64},{192,128},{1,193},{65,1},{129,65},{193,129... | collective-permute-start | bytes 638984 | tf_op jit(solution)/shard_map/ppermute | solution.py:314
  (23 other events, 71.7 us)
